TPU v7x, 256 devices: a whole 4x4x8 slice. The times are simulated.
256 devices in a mesh: row: 8 (over z_hi, x), col: 32 (over z_lo, y, core).
Axes of the slice: x: 4, y: 4, z: 8 (z_hi: 2, z_lo: 4; z = z_hi * 4 + z_lo), core: 2. Of those that a mesh axis runs over, the one named last changes fastest.
Arguments:
- object_field: float32 [2, 2048, 8192], P(None, 'row', 'col'), may hold values from -6 to 6
- probe: float32 [2, 4, 128, 128], replicated, may hold values from -6 to 6
- patterns: bfloat16 [8, 32, 8, 128, 128], P('row', 'col'), may hold values from 0.5 to 2
- row_scales: float32 [8, 32, 8, 128], P('row', 'col'), may hold values from 0.3 to 3
- positions: int32 [8, 32, 8, 2], P('row', 'col'), may hold values from 0 to 255
- counts: int32 [8, 32], P('row', 'col'), may hold values from 4 to 8, as said below
Outputs:
- object_out: float32 [2, 2048, 8192], P(None, 'row', 'col')
- probe_out: float32 [2, 4, 128, 128], replicated
Inputs may be any that keep to these rules, and one draw needn't show every extreme that they name: positions p >= counts[a,b] of tile (a,b) are ignored; some tile has all 8 positions live.
All inputs are finite; a program needn't handle non-finite values.
Results may differ from a plain program's by a relative error of at most 0.0003.
Values sent between devices are 32-bit elements; how exact they have to be, the bound alone decides.
No kernel may reach another device: no remote copies, remote signals or barrier semaphores. Data moves between devices by JAX's collectives and lax.ppermute only.
A program may use at most 128 MiB of HBM per device.

v0:
```python
import math

import jax
import jax.numpy as jnp
from jax import lax
from jax.sharding import PartitionSpec as P

PASSES = 2


def padded_2(block, sides, width):
    for axis, dim in sides:
        count = lax.axis_size(axis)
        forward = [(i, i + 1) for i in range(count - 1)]
        backward = [(target, source) for source, target in forward]
        low = lax.ppermute(
            lax.slice_in_dim(block, block.shape[dim] - width, None, axis=dim), axis, forward
        )
        high = lax.ppermute(lax.slice_in_dim(block, 0, width, axis=dim), axis, backward)
        block = jnp.concatenate([low, block, high], axis=dim)
    return block


def dft_tables(length):
    indices = lax.iota(jnp.int32, length)
    product = indices[:, None] * indices[None, :] % length
    angle = product.astype(jnp.float32) * (2.0 * math.pi / length)
    scaling = 1.0 / math.sqrt(length)
    cosine = jnp.cos(angle) * scaling
    sine_part = jnp.sin(angle) * scaling
    forward = jnp.concatenate(
        [jnp.concatenate([cosine, -sine_part], 1), jnp.concatenate([sine_part, cosine], 1)], 0
    )
    inverse = jnp.concatenate(
        [jnp.concatenate([cosine, sine_part], 1), jnp.concatenate([-sine_part, cosine], 1)], 0
    )
    return (forward, inverse)


def apply_table(waves, table):
    flattened = waves.reshape(-1, table.shape[0])
    result = jnp.dot(
        flattened, table, precision=lax.Precision.HIGHEST, preferred_element_type=jnp.float32
    )
    return result.reshape(waves.shape)


def transpose_pairs(waves):
    batch_size, length, pair_width = waves.shape
    return (
        waves.reshape(batch_size, length, 2, length)
        .transpose(0, 3, 2, 1)
        .reshape(batch_size, length, pair_width)
    )


def transform(waves, table):
    return transpose_pairs(apply_table(transpose_pairs(apply_table(waves, table)), table))


def fold_rim(padded, axis_number, inner, rim_width):
    middle = lax.slice_in_dim(padded, 2 * rim_width, 2 * rim_width + inner, axis=axis_number)
    lower = lax.slice_in_dim(padded, 0, rim_width, axis=axis_number)
    upper = lax.slice_in_dim(padded, inner + 3 * rim_width, inner + 4 * rim_width, axis=axis_number)
    head_part = lax.slice_in_dim(middle, 0, rim_width, axis=axis_number) + lower
    core_part = lax.slice_in_dim(middle, rim_width, inner - rim_width, axis=axis_number)
    tail_part = lax.slice_in_dim(middle, inner - rim_width, inner, axis=axis_number) + upper
    return jnp.concatenate([head_part, core_part, tail_part], axis=axis_number)


def on_device(object_field, probe, patterns, row_scales, positions, counts):
    modes = probe.shape[1]
    pattern_size = probe.shape[2]
    rim_width = pattern_size // 2
    tile_rows = object_field.shape[1]
    tile_cols = object_field.shape[2]
    position_count = positions.shape[2]
    forward, inverse = dft_tables(pattern_size)
    amplitudes = patterns[0, 0].astype(jnp.float32) * row_scales[0, 0][..., None]
    starts = positions[0, 0]
    live_flag = (lax.iota(jnp.int32, position_count) < counts[0, 0]).astype(jnp.float32)
    object_now = object_field
    probe_now = probe
    for pass_number in range(PASSES):
        extended = padded_2(object_now, (("row", 1), ("col", 2)), rim_width)
        patches = jax.vmap(
            lambda start_pair: lax.dynamic_slice(
                extended, (0, start_pair[0], start_pair[1]), (2, pattern_size, pattern_size)
            )
        )(starts)
        patch_re = patches[:, 0][:, None]
        patch_im = patches[:, 1][:, None]
        probe_re = probe_now[0][None]
        probe_im = probe_now[1][None]
        wave_re = probe_re * patch_re - probe_im * patch_im
        wave_im = probe_re * patch_im + probe_im * patch_re
        stacked = jnp.concatenate([wave_re, wave_im], axis=-1).reshape(
            -1, pattern_size, 2 * pattern_size
        )
        far_field = transform(stacked, forward).reshape(
            position_count, modes, pattern_size, 2 * pattern_size
        )
        far_re = far_field[..., :pattern_size]
        far_im = far_field[..., pattern_size:]
        intensity = jnp.sum(far_re * far_re + far_im * far_im, axis=1, keepdims=True)
        factor = amplitudes[:, None] / jnp.maximum(jnp.sqrt(intensity), 0.5)
        scaled = far_field * jnp.concatenate([factor, factor], axis=-1)
        back_wave = transform(scaled.reshape(-1, pattern_size, 2 * pattern_size), inverse)
        back_wave = back_wave.reshape(position_count, modes, pattern_size, 2 * pattern_size)
        live_mask = live_flag[:, None, None, None]
        diff_re = (back_wave[..., :pattern_size] - wave_re) * live_mask
        diff_im = (back_wave[..., pattern_size:] - wave_im) * live_mask
        contrib_re = jnp.sum(probe_re * diff_re + probe_im * diff_im, axis=1)
        contrib_im = jnp.sum(probe_re * diff_im - probe_im * diff_re, axis=1)
        updates = jnp.zeros((2, tile_rows + 2 * rim_width, tile_cols + 2 * rim_width), jnp.float32)
        for position in range(position_count):
            corner = (0, starts[position, 0], starts[position, 1])
            current = lax.dynamic_slice(updates, corner, (2, pattern_size, pattern_size))
            contribution = jnp.stack([contrib_re[position], contrib_im[position]])
            updates = lax.dynamic_update_slice(updates, current + contribution, corner)
        gradient_re = jnp.sum(patch_re * diff_re + patch_im * diff_im, axis=0)
        gradient_im = jnp.sum(patch_re * diff_im - patch_im * diff_re, axis=0)
        gradient = jnp.stack([gradient_re, gradient_im])
        weight = jnp.sum(
            live_flag[:, None, None] * (patches[:, 0] ** 2 + patches[:, 1] ** 2), axis=0
        )
        summed = padded_2(updates, (("row", 1), ("col", 2)), rim_width)
        tile_sum = fold_rim(fold_rim(summed, 1, tile_rows, rim_width), 2, tile_cols, rim_width)
        probe_peak = jnp.max(jnp.sum(probe_now[0] ** 2 + probe_now[1] ** 2, axis=0))
        object_now = object_now + tile_sum / probe_peak
        gradient_sum, weight_sum = lax.psum((gradient, weight), ("row", "col"))
        probe_now = probe_now + gradient_sum / weight_sum[None, None]
    return (object_now, probe_now)


def solution(mesh):
    placed = (
        P(None, "row", "col"),
        P(),
        P("row", "col", None, None, None),
        P("row", "col", None, None),
        P("row", "col", None, None),
        P("row", "col"),
    )
    return jax.shard_map(
        on_device,
        mesh=mesh,
        in_specs=placed,
        out_specs=(P(None, "row", "col"), P()),
        check_vma=False,
    )
```

profile of v0, /device:TPU:63, one launch (start us, length us, event | category | flops | bytes accessed | tf_op | source)
XLA Modules:
  0.0 853.0 jit_solution(2227831163460324998)
XLA Ops:
  8.2 7.8 collective-permute-start
  54.9 3.1 collective-permute-start.2
  62.7 6.5 collective-permute-done.3
  70.7 24.4 %while.2 = (s32[]{:T(128)}, f32[2,384,384]{2,1,0:T(8,128)}, s32[8,3]{0,1:T(4,128)S(1)}, f32[8,2,128,128]{3,2,0,1:T(8,128)S(1)}, s32[]{:T(128)}) while((s32[]{:T(128)}, f32[2,384,384]{2,1,0:T(8,128)}, s32[8,3]{0,1:T(4,128)S(1)}, f32[8,2,128,128]{3,2,0,1:T(8,128)S(1)}, s32[]{:T(128)}) %tuple.107), condition=%wide.while_cond, body=%wide.while_body.sunk | while | flops 2 | bytes 262261 | solution.py:87
  96.5 3.7 fusion
  100.2 7.1 fusion.47
  110.3 7.1 fusion.48
  117.4 7.3 fusion.49
  131.8 4.9 add_reduce_fusion.2
  156.5 10.5 %collective-permute-start.4 = (f32[2,64,384]{2,1,0:T(8,128)S(1)}, f32[2,64,384]{2,1,0:T(8,128)S(1)}, u32[]{:S(2)}, u32[]{:S(2)}) collective-permute-start(f32[2,64,384]{2,1,0:T(8,128)S(1)} %get-tuple-element.66), channel_id=1, source_target_pairs={{0,32},{32,64},{64,96},{96,128},{128,160},{160,192},{192,224},{1,3... | collective-permute-start | bytes 589832 | tf_op jit(solution)/shard_map/ppermute | solution.py:16
  170.9 10.1 %collective-permute-done.5 = f32[2,64,384]{2,1,0:T(8,128)S(1)} collective-permute-done((f32[2,64,384]{2,1,0:T(8,128)S(1)}, f32[2,64,384]{2,1,0:T(8,128)S(1)}, u32[]{:S(2)}, u32[]{:S(2)}) %collective-permute-start.5) | collective-permute-done | bytes 196640 | tf_op jit(solution)/shard_map/ppermute | solution.py:19
  182.1 4.1 collective-permute-start.6
  188.9 3.8 collective-permute-done.6
  192.7 6.5 collective-permute-done.7
  206.7 3.4 collective-permute-start.9
  210.5 7.9 collective-permute-done.9
  219.4 3.8 collective-permute-start.10
  228.3 6.5 collective-permute-done.11
  237.4 28.9 %while.3 = (s32[]{:T(128)}, f32[2,384,384]{2,1,0:T(8,128)}, s32[8,3]{0,1:T(4,128)S(1)}, f32[8,2,128,128]{3,2,1,0:T(8,128)}, s32[]{:T(128)}) while((s32[]{:T(128)}, f32[2,384,384]{2,1,0:T(8,128)}, s32[8,3]{0,1:T(4,128)S(1)}, f32[8,2,128,128]{3,2,1,0:T(8,128)}, s32[]{:T(128)}) %tuple.119), condition=%wide.while_cond.1, body=%wide.while_body.1.sunk | while | flops 2 | bytes 263785 | solution.py:87
  252.5 3.0 bitcast_dynamic-update-slice_fusion.5
  263.3 3.0 bitcast_dynamic-update-slice_fusion.5
  271.3 244.9 %all-reduce.7.cloned.1.call-done = (f32[2,4,128,128]{3,2,1,0:T(8,128)}, f32[128,128]{1,0:T(8,128)}) async-done(((f32[2,4,128,128]{3,2,1,0:T(8,128)}, f32[128,128]{1,0:T(8,128)}), (f32[2,4,128,128]{3,2,1,0:T(8,128)}, f32[128,128]{1,0:T(8,128)})) %all-reduce.7.cloned.1.call-update) | async-done | bytes 589840 | tf_op jit(solution)/shard_map/psum | solution.py:131
  518.2 3.7 fusion.3
  521.9 7.1 fusion.50
  531.5 7.1 fusion.51
  538.6 7.4 fusion.52
  553.1 4.8 add_reduce_fusion
  578.3 5.2 collective-permute-start.12
  587.0 4.5 collective-permute-done.12
  591.5 9.5 %collective-permute-done.13 = f32[2,64,384]{2,1,0:T(8,128)S(1)} collective-permute-done((f32[2,64,384]{2,1,0:T(8,128)S(1)}, f32[2,64,384]{2,1,0:T(8,128)S(1)}, u32[]{:S(2)}, u32[]{:S(2)}) %collective-permute-start.13) | collective-permute-done | bytes 196640 | tf_op jit(solution)/shard_map/ppermute | solution.py:19
  602.2 5.8 collective-permute-start.14
  609.9 231.2 %all-reduce.5.cloned.1.call-done = (f32[2,4,128,128]{3,2,1,0:T(8,128)}, f32[128,128]{1,0:T(8,128)}) async-done(((f32[2,4,128,128]{3,2,1,0:T(8,128)}, f32[128,128]{1,0:T(8,128)}), (f32[2,4,128,128]{3,2,1,0:T(8,128)}, f32[128,128]{1,0:T(8,128)})) %all-reduce.5.cloned.1.call-update) | async-done | bytes 589840 | tf_op jit(solution)/shard_map/psum | solution.py:131
  (213 shorter events, 164.5 us)
Async XLA Ops:
  7.2 509.0 %all-reduce.7.cloned.1.call-start = ((), (), s32[]{:S(2)}) async-start(), calls=%async_computation.1 | async-start | bytes 1179648 | tf_op jit(solution)/shard_map/psum | solution.py:131
  8.2 45.3 %collective-permute-start = (f32[2,64,256]{2,1,0:T(8,128)S(1)}, f32[2,64,256]{2,1,0:T(8,128)S(1)}, u32[]{:S(2)}, u32[]{:S(2)}) collective-permute-start(f32[2,64,256]{2,1,0:T(8,128)S(1)} %get-tuple-element.117), channel_id=1, source_target_pairs={{0,32},{32,64},{64,96},{96,128},{128,160},{160,192},{192,224},{1,3... | collective-permute-start | bytes 393224 | tf_op jit(solution)/shard_map/ppermute | solution.py:16
  16.0 38.6 %collective-permute-start.1 = (f32[2,64,256]{2,1,0:T(8,128)S(1)}, f32[2,64,256]{2,1,0:T(8,128)S(1)}, u32[]{:S(2)}, u32[]{:S(2)}) collective-permute-start(f32[2,64,256]{2,1,0:T(8,128)S(1)} %get-tuple-element.116), channel_id=1, source_target_pairs={{32,0},{64,32},{96,64},{128,96},{160,128},{192,160},{224,192},{33,... | collective-permute-start | bytes 393224 | tf_op jit(solution)/shard_map/ppermute | solution.py:19
  42.2 17.8 %copy-start = (f32[2,4,128,128]{3,2,1,0:T(8,128)S(1)}, f32[2,4,128,128]{3,2,1,0:T(8,128)}, u32[]{:S(2)}) copy-start(f32[2,4,128,128]{3,2,1,0:T(8,128)} %param.7) | copy-start | bytes 1572868
  54.9 7.9 collective-permute-start.2
  58.0 11.2 %collective-permute-start.3 = (f32[2,384,64]{2,1,0:T(8,128)S(1)}, f32[2,384,64]{2,1,0:T(8,128)S(1)}, u32[]{:S(2)}, u32[]{:S(2)}) collective-permute-start(f32[2,384,64]{2,1,0:T(8,128)S(1)} %get-tuple-element.77), channel_id=1, source_target_pairs={{1,0},{2,1},{3,2},{4,3},{5,4},{6,5},{7,6},{8,7},{9,8},{10,9},{11,1... | collective-permute-start | bytes 589832 | tf_op jit(solution)/shard_map/ppermute | solution.py:19
  60.7 34.6 %copy-start.10 = (f32[4,128,128]{2,1,0:T(8,128)}, f32[4,128,128]{2,1,0:T(8,128)S(1)}, u32[]{:S(2)}) copy-start(f32[4,128,128]{2,1,0:T(8,128)S(1)} %get-tuple-element.114) | copy-start | bytes 786436
  70.7 24.6 %copy-start.11 = (f32[4,128,128]{2,1,0:T(8,128)S(1)}, f32[4,128,128]{2,1,0:T(8,128)}, u32[]{:S(2)}) copy-start(f32[4,128,128]{2,1,0:T(8,128)} %get-tuple-element.115) | copy-start | bytes 786436
  95.3 1.2 copy-start.4
  156.5 14.4 %collective-permute-start.4 = (f32[2,64,384]{2,1,0:T(8,128)S(1)}, f32[2,64,384]{2,1,0:T(8,128)S(1)}, u32[]{:S(2)}, u32[]{:S(2)}) collective-permute-start(f32[2,64,384]{2,1,0:T(8,128)S(1)} %get-tuple-element.66), channel_id=1, source_target_pairs={{0,32},{32,64},{64,96},{96,128},{128,160},{160,192},{192,224},{1,3... | collective-permute-start | bytes 589832 | tf_op jit(solution)/shard_map/ppermute | solution.py:16
  167.0 14.0 %collective-permute-start.5 = (f32[2,64,384]{2,1,0:T(8,128)S(1)}, f32[2,64,384]{2,1,0:T(8,128)S(1)}, u32[]{:S(2)}, u32[]{:S(2)}) collective-permute-start(f32[2,64,384]{2,1,0:T(8,128)S(1)} %get-tuple-element.67), channel_id=1, source_target_pairs={{32,0},{64,32},{96,64},{128,96},{160,128},{192,160},{224,192},{33,... | collective-permute-start | bytes 589832 | tf_op jit(solution)/shard_map/ppermute | solution.py:19
  182.1 10.6 %collective-permute-start.6 = (f32[2,512,64]{2,1,0:T(8,128)}, f32[2,512,64]{2,1,0:T(8,128)S(1)}, u32[]{:S(2)}, u32[]{:S(2)}) collective-permute-start(f32[2,512,64]{2,1,0:T(8,128)} %get-tuple-element.60), channel_id=1, source_target_pairs={{0,1},{1,2},{2,3},{3,4},{4,5},{5,6},{6,7},{7,8},{8,9},{9,10},{10,1... | collective-permute-start | bytes 786440 | tf_op jit(solution)/shard_map/ppermute | solution.py:16
  186.3 12.9 %collective-permute-start.7 = (f32[2,512,64]{2,1,0:T(8,128)}, f32[2,512,64]{2,1,0:T(8,128)}, u32[]{:S(2)}, u32[]{:S(2)}) collective-permute-start(f32[2,512,64]{2,1,0:T(8,128)} %get-tuple-element.61), channel_id=1, source_target_pairs={{1,0},{2,1},{3,2},{4,3},{5,4},{6,5},{7,6},{8,7},{9,8},{10,9},{11,1... | collective-permute-start | bytes 786440 | tf_op jit(solution)/shard_map/ppermute | solution.py:19
  204.6 20.7 %copy-start.15 = (f32[4,128,128]{2,1,0:T(8,128)S(1)}, f32[4,128,128]{2,1,0:T(8,128)}, u32[]{:S(2)}) copy-start(f32[4,128,128]{2,1,0:T(8,128)} %get-tuple-element.22) | copy-start | bytes 786436
  204.6 20.7 %copy-start.16 = (f32[4,128,128]{2,1,0:T(8,128)S(1)}, f32[4,128,128]{2,1,0:T(8,128)}, u32[]{:S(2)}) copy-start(f32[4,128,128]{2,1,0:T(8,128)} %get-tuple-element.25) | copy-start | bytes 786436
  204.6 5.8 collective-permute-start.8
  206.7 11.7 %collective-permute-start.9 = (f32[2,64,256]{2,1,0:T(8,128)S(1)}, f32[2,64,256]{2,1,0:T(8,128)S(1)}, u32[]{:S(2)}, u32[]{:S(2)}) collective-permute-start(f32[2,64,256]{2,1,0:T(8,128)S(1)} %get-tuple-element.97), channel_id=1, source_target_pairs={{32,0},{64,32},{96,64},{128,96},{160,128},{192,160},{224,192},{33,... | collective-permute-start | bytes 393224 | tf_op jit(solution)/shard_map/ppermute | solution.py:19
  219.4 8.8 %collective-permute-start.10 = (f32[2,384,64]{2,1,0:T(8,128)}, f32[2,384,64]{2,1,0:T(8,128)}, u32[]{:S(2)}, u32[]{:S(2)}) collective-permute-start(f32[2,384,64]{2,1,0:T(8,128)} %get-tuple-element.74), channel_id=1, source_target_pairs={{0,1},{1,2},{2,3},{3,4},{4,5},{5,6},{6,7},{7,8},{8,9},{9,10},{10,1... | collective-permute-start | bytes 589832 | tf_op jit(solution)/shard_map/ppermute | solution.py:16
  223.3 11.5 %collective-permute-start.11 = (f32[2,384,64]{2,1,0:T(8,128)}, f32[2,384,64]{2,1,0:T(8,128)}, u32[]{:S(2)}, u32[]{:S(2)}) collective-permute-start(f32[2,384,64]{2,1,0:T(8,128)} %get-tuple-element.75), channel_id=1, source_target_pairs={{1,0},{2,1},{3,2},{4,3},{5,4},{6,5},{7,6},{8,7},{9,8},{10,9},{11,1... | collective-permute-start | bytes 589832 | tf_op jit(solution)/shard_map/ppermute | solution.py:19
  226.1 40.3 %copy-start.6 = (f32[8,2,128,128]{3,2,0,1:T(8,128)S(1)}, f32[8,2,128,128]{3,2,0,1:T(8,128)}, u32[]{:S(2)}) copy-start(f32[8,2,128,128]{3,2,0,1:T(8,128)} %copy-done.5) | copy-start | bytes 3145732
  268.5 572.7 %all-reduce.5.cloned.1.call-start = ((), (), s32[]{:S(2)}) async-start(), calls=%async_computation | async-start | bytes 1179648 | tf_op jit(solution)/shard_map/psum | solution.py:131
  270.0 247.9 %copy-start.1 = (f32[8,128,128]{2,1,0:T(8,128)}, f32[8,128,128]{2,1,0:T(8,128)S(1)}, u32[]{:S(2)}) copy-start(f32[8,128,128]{2,1,0:T(8,128)S(1)} %slice_bitcast_fusion) | copy-start | bytes 1572868
  271.3 246.7 %copy-start.2 = (f32[8,128,128]{2,1,0:T(8,128)}, f32[8,128,128]{2,1,0:T(8,128)S(1)}, u32[]{:S(2)}) copy-start(f32[8,128,128]{2,1,0:T(8,128)S(1)} %slice_bitcast_fusion.1) | copy-start | bytes 1572868
  550.2 3.0 copy-start.13
  565.4 20.0 %copy-start.17 = (f32[4,128,128]{2,1,0:T(8,128)S(1)}, f32[4,128,128]{2,1,0:T(8,128)}, u32[]{:S(2)}) copy-start(f32[4,128,128]{2,1,0:T(8,128)} %get-tuple-element.18) | copy-start | bytes 786436
  565.4 20.0 %copy-start.18 = (f32[4,128,128]{2,1,0:T(8,128)S(1)}, f32[4,128,128]{2,1,0:T(8,128)}, u32[]{:S(2)}) copy-start(f32[4,128,128]{2,1,0:T(8,128)} %get-tuple-element.21) | copy-start | bytes 786436
  578.3 13.2 %collective-permute-start.12 = (f32[2,64,384]{2,1,0:T(8,128)}, f32[2,64,384]{2,1,0:T(8,128)S(1)}, u32[]{:S(2)}, u32[]{:S(2)}) collective-permute-start(f32[2,64,384]{2,1,0:T(8,128)} %get-tuple-element.64), channel_id=1, source_target_pairs={{0,32},{32,64},{64,96},{96,128},{128,160},{160,192},{192,224},{1,3... | collective-permute-start | bytes 589832 | tf_op jit(solution)/shard_map/ppermute | solution.py:16
  583.5 17.6 %collective-permute-start.13 = (f32[2,64,384]{2,1,0:T(8,128)S(1)}, f32[2,64,384]{2,1,0:T(8,128)S(1)}, u32[]{:S(2)}, u32[]{:S(2)}) collective-permute-start(f32[2,64,384]{2,1,0:T(8,128)S(1)} %get-tuple-element.65), channel_id=1, source_target_pairs={{32,0},{64,32},{96,64},{128,96},{160,128},{192,160},{224,192},{33,... | collective-permute-start | bytes 589832 | tf_op jit(solution)/shard_map/ppermute | solution.py:19
  601.1 1.1 copy-start.8
  602.2 240.9 %collective-permute-start.14 = (f32[2,512,64]{2,1,0:T(8,128)}, f32[2,512,64]{2,1,0:T(8,128)S(1)}, u32[]{:S(2)}, u32[]{:S(2)}) collective-permute-start(f32[2,512,64]{2,1,0:T(8,128)} %get-tuple-element.56), channel_id=1, source_target_pairs={{0,1},{1,2},{2,3},{3,4},{4,5},{5,6},{6,7},{7,8},{8,9},{9,10},{10,1... | collective-permute-start | bytes 786440 | tf_op jit(solution)/shard_map/ppermute | solution.py:16
  608.0 235.1 %collective-permute-start.15 = (f32[2,512,64]{2,1,0:T(8,128)}, f32[2,512,64]{2,1,0:T(8,128)S(1)}, u32[]{:S(2)}, u32[]{:S(2)}) collective-permute-start(f32[2,512,64]{2,1,0:T(8,128)} %get-tuple-element.57), channel_id=1, source_target_pairs={{1,0},{2,1},{3,2},{4,3},{5,4},{6,5},{7,6},{8,7},{9,8},{10,9},{11,1... | collective-permute-start | bytes 786440 | tf_op jit(solution)/shard_map/ppermute | solution.py:19
  841.2 2.2 copy-start.9
  (6 other events, 5.3 us)
Sparse Core Ops, SparseCore 0:
  268.6 247.5 all-reduce.6
  586.4 254.7 all-reduce.4
where the time goes:
time: 862 us; the launch traced here: 853 us
  waiting for transfers between devices  538 us (62%)
  local copies, waits for them, and re-layouts  118 us (14%)
  starting transfers between devices  59.7 us (7%)
  matrix products  50.5 us (6%)
  between operations  46.7 us (5%)
  other arithmetic  39.4 us (5%)
    psum x2, waiting for transfers between devices, on_device(): gradient_sum, weight_sum = lax.psum((gradient, weight), ('row', 'col'))  476 us
    gather x48, local copies, waits for them, and re-layouts  53.1 us
    dot_general x8, matrix products, apply_table(): jnp.dot(flattened, table, precision=lax.Precision.HIGHEST, preferred_elem...  50.5 us
    ppermute x8, waiting for transfers between devices, padded_2(): lax.ppermute(lax.slice_in_dim(block, 0, width, axis=dim), axis, backward)  47.1 us
    ppermute x8, starting transfers between devices, padded_2(): lax.ppermute(lax.slice_in_dim(block, block.shape[dim] - width, None, axis...  42.4 us
    dynamic_update_slice x16, local copies, waits for them, and re-layouts, on_device(): updates = lax.dynamic_update_slice(updates, current + contribution, corner)  37.1 us
  transfers between devices with their start and end apart: 18, of which 14 were waited for; matrix products, arithmetic and copies ran while one was open for 2% of the time, Pallas kernels for 0%

commit v1 on v0

v1 whole, which is shorter than its diff:
```python
import functools

import numpy as np

import jax
import jax.numpy as jnp
from jax import lax
from jax.experimental import pallas as pl
from jax.experimental.pallas import tpu as pltpu
from jax.sharding import PartitionSpec as P

LANES = 128
SUBLANES = 8


def dft_tables(length):
    index = np.arange(length)
    angle = (np.outer(index, index) % length) * (2.0 * np.pi / length)
    cosine = np.cos(angle) / np.sqrt(length)
    sine = np.sin(angle) / np.sqrt(length)
    forward = np.block([[cosine, -sine], [sine, cosine]]).astype(np.float32)
    high = forward.astype(jnp.bfloat16)
    low = (forward - high.astype(np.float32)).astype(jnp.bfloat16)
    return high, low, np.ascontiguousarray(high.T), np.ascontiguousarray(low.T)


def split(value):
    high = value.astype(jnp.bfloat16)
    low = (value - high.astype(jnp.float32)).astype(jnp.bfloat16)
    return high, low


def mm(left, right):
    return jnp.dot(left, right, preferred_element_type=jnp.float32)


def product(left, right):
    (lh, ll), (rh, rl) = left, right
    return mm(lh, rh) + (mm(lh, rl) + mm(ll, rh))


def pass_kernel(
    starts, counts, frame, probe, amplitude, fh, fl, ih, il, updates, sums, *, modes, size, margin
):
    updates[...] = jnp.zeros_like(updates)
    sums[...] = jnp.zeros_like(sums)
    forward = (fh[...], fl[...])
    inverse = (ih[...], il[...])

    def position(p, carry):
        row = starts[p, 0]
        col = starts[p, 1] + margin
        base = pl.multiple_of(col // LANES * LANES, LANES)
        shift = col % LANES
        tall, wide = size + SUBLANES, 2 * size
        down = row % SUBLANES
        rows = pl.ds(pl.multiple_of(row // SUBLANES * SUBLANES, SUBLANES), tall)
        cols = pl.ds(base, wide)

        def cut(window):
            window = pltpu.roll(window, lax.rem(wide - shift, wide), 1)[:, :size]
            return pltpu.roll(window, lax.rem(tall - down, tall), 0)[:size]

        def placed(patch):
            patch = jnp.concatenate([patch, jnp.zeros((SUBLANES, size), jnp.float32)], axis=0)
            patch = pltpu.roll(patch, down, 0)
            return pltpu.roll(jnp.concatenate([patch, jnp.zeros_like(patch)], axis=1), shift, 1)

        patch_re = cut(frame[0, rows, cols])
        patch_im = cut(frame[1, rows, cols])
        waves = []
        for m in range(modes):
            pr, pi = probe[0, m], probe[1, m]
            waves.append((pr * patch_re - pi * patch_im, pr * patch_im + pi * patch_re))
        stacked = jnp.concatenate([jnp.concatenate(w, axis=1) for w in waves], axis=0)
        half = product(split(stacked), forward)
        blocks = [half[m * size : (m + 1) * size] for m in range(modes)]
        side = jnp.concatenate(
            [jnp.concatenate([b[:, :size], b[:, size:]], axis=0) for b in blocks], axis=1
        )
        far = product(inverse, split(side))
        squares = far * far
        power = squares[:size] + squares[size:]
        intensity = power[:, :size]
        for m in range(1, modes):
            intensity = intensity + power[:, m * size : (m + 1) * size]
        factor = amplitude[p] / jnp.maximum(jnp.sqrt(intensity), 0.5)
        wide = jnp.concatenate([factor] * modes, axis=1)
        scaled = far * jnp.concatenate([wide, wide], axis=0)
        half = product(forward, split(scaled))
        stacked = jnp.concatenate(
            [
                jnp.concatenate(
                    [half[:size, m * size : (m + 1) * size], half[size:, m * size : (m + 1) * size]],
                    axis=1,
                )
                for m in range(modes)
            ],
            axis=0,
        )
        back = product(split(stacked), inverse)
        total_re = total_im = None
        for m in range(modes):
            pr, pi = probe[0, m], probe[1, m]
            dr = back[m * size : (m + 1) * size, :size] - waves[m][0]
            di = back[m * size : (m + 1) * size, size:] - waves[m][1]
            sums[m] += patch_re * dr + patch_im * di
            sums[modes + m] += patch_re * di - patch_im * dr
            add_re = pr * dr + pi * di
            add_im = pr * di - pi * dr
            total_re = add_re if m == 0 else total_re + add_re
            total_im = add_im if m == 0 else total_im + add_im
        sums[2 * modes] += patch_re * patch_re + patch_im * patch_im
        updates[0, rows, cols] += placed(total_re)
        updates[1, rows, cols] += placed(total_im)
        return carry

    lax.fori_loop(0, counts[0], position, 0)
    strength = probe[0, 0] * probe[0, 0] + probe[1, 0] * probe[1, 0]
    for m in range(1, modes):
        strength = strength + probe[0, m] * probe[0, m] + probe[1, m] * probe[1, m]
    updates[...] = updates[...] / jnp.max(strength)


def run_pass(starts, count, frame, probe, amplitude, tables, margin):
    modes, size = probe.shape[1], probe.shape[2]
    vmem = pl.BlockSpec(memory_space=pltpu.VMEM)
    smem = pl.BlockSpec(memory_space=pltpu.SMEM)
    flops = 24 * starts.shape[0] * modes * size * (2 * size) ** 2
    return pl.pallas_call(
        functools.partial(pass_kernel, modes=modes, size=size, margin=margin),
        out_shape=(
            jax.ShapeDtypeStruct(frame.shape, jnp.float32),
            jax.ShapeDtypeStruct((2 * modes + 1, size, size), jnp.float32),
        ),
        in_specs=[smem, smem] + [vmem] * 7,
        out_specs=(vmem, vmem),
        cost_estimate=pl.CostEstimate(flops=flops, bytes_accessed=6 << 20, transcendentals=0),
        compiler_params=pltpu.CompilerParams(vmem_limit_bytes=48 << 20),
    )(starts, count, frame, probe, amplitude, *tables)


def neighbours(low_strip, high_strip, axis):
    count = lax.axis_size(axis)
    up = [(i, i + 1) for i in range(count - 1)]
    down = [(i + 1, i) for i in range(count - 1)]
    return lax.ppermute(high_strip, axis, up), lax.ppermute(low_strip, axis, down)


def spread(chunk, axis):
    count = lax.axis_size(axis)
    return lax.all_to_all(jnp.broadcast_to(chunk[None], (count, *chunk.shape)), axis, 0, 0, tiled=True)


def total(sums):
    count = lax.axis_size("col")
    parts = lax.all_to_all(sums.reshape(count, -1, LANES), "col", 0, 0, tiled=True)
    part = jnp.sum(spread(jnp.sum(parts, axis=0), "row"), axis=0)
    return spread(part, "col").reshape(sums.shape)


def at(array, dim, start, stop):
    return lax.slice_in_dim(array, start, stop, axis=dim)


def padded(array, dim, low, size):
    pads = [(0, 0, 0)] * array.ndim
    pads[dim] = (low, size - low - array.shape[dim], 0)
    return lax.pad(array, jnp.float32(0), pads)


def on_device(object_field, probe, patterns, row_scales, positions, counts):
    modes, size = probe.shape[1], probe.shape[2]
    rim = size // 2
    rows, cols = object_field.shape[1:]
    tall, wide = rows + 2 * rim, cols + 2 * LANES
    margin = LANES - rim
    tables = [jnp.asarray(t) for t in dft_tables(size)]
    amplitude = patterns[0, 0].astype(jnp.float32) * row_scales[0, 0][..., None]
    starts, count = positions[0, 0], counts[0]

    low, high = neighbours(at(object_field, 1, 0, rim), at(object_field, 1, rows - rim, rows), "row")
    frame = jnp.concatenate([low, object_field, high], axis=1)
    low, high = neighbours(at(frame, 2, 0, LANES), at(frame, 2, cols - LANES, cols), "col")
    frame = jnp.concatenate([low, frame, high], axis=2)

    updates, sums = run_pass(starts, count, frame, probe, amplitude, tables, margin)
    low, high = neighbours(at(updates, 1, 0, 2 * rim), at(updates, 1, rows, tall), "row")
    updates = updates + padded(low, 1, 0, tall) + padded(high, 1, rows, tall)
    left = margin, margin + 2 * rim
    right = margin + cols, margin + cols + 2 * rim
    low, high = neighbours(at(updates, 2, *left), at(updates, 2, *right), "col")
    updates = updates + padded(low, 2, margin, wide) + padded(high, 2, margin + cols, wide)
    at_row = lax.broadcasted_iota(jnp.int32, (1, tall, 1), 1) + (lax.axis_index("row") * rows - rim)
    at_col = lax.broadcasted_iota(jnp.int32, (1, 1, wide), 2) + (lax.axis_index("col") * cols - LANES)
    inside = (at_row >= 0) & (at_row < rows * lax.axis_size("row"))
    inside = inside & (at_col >= 0) & (at_col < cols * lax.axis_size("col"))
    frame = frame + jnp.where(inside, updates, 0.0)
    sums = total(sums)
    probe = probe + sums[: 2 * modes].reshape(probe.shape) / sums[2 * modes]

    updates, sums = run_pass(starts, count, frame, probe, amplitude, tables, margin)
    low, high = neighbours(at(updates, 1, 0, rim), at(updates, 1, tall - rim, tall), "row")
    middle = at(updates, 1, rim, rim + rows)
    middle = middle + padded(low, 1, 0, rows) + padded(high, 1, rows - rim, rows)
    low, high = neighbours(
        at(middle, 2, margin, LANES), at(middle, 2, LANES + cols, wide - margin), "col"
    )
    tile = at(middle, 2, LANES, LANES + cols)
    tile = tile + padded(low, 2, 0, cols) + padded(high, 2, cols - rim, cols)
    object_out = frame[:, rim : rim + rows, LANES : LANES + cols] + tile
    sums = total(sums)
    probe_out = probe + sums[: 2 * modes].reshape(probe.shape) / sums[2 * modes]
    return object_out, probe_out


def solution(mesh):
    placed = (
        P(None, "row", "col"),
        P(),
        P("row", "col", None, None, None),
        P("row", "col", None, None),
        P("row", "col", None, None),
        P("row", "col"),
    )
    return jax.shard_map(
        on_device,
        mesh=mesh,
        in_specs=placed,
        out_specs=(P(None, "row", "col"), P()),
        check_vma=False,
    )
```

time: 862 us -> 243 us (0.28)
  waiting for transfers between devices: 538 us -> 75.1 us
  local copies, waits for them, and re-layouts: 118 us -> 16.4 us
  matrix products: 50.5 us -> 0 us
  between operations: 46.7 us -> 1.75 us
  Pallas kernels: 0 us -> 30.6 us
  other arithmetic: 39.4 us -> 11.2 us
  starting transfers between devices: 59.7 us -> 85 us
  blocking collectives: 0 us -> 21 us
    psum x2 -> x0, waiting for transfers between devices: 476 us -> none  [on_device(): gradient_sum, weight_sum = lax.psum((gradient, weight), ('row', 'col'))]
    gather x48 -> x0, local copies, waits for them, and re-layouts: 53.1 us -> none
    dot_general x8 -> x0, matrix products: 50.5 us -> none  [apply_table(): jnp.dot(flattened, table, precision=lax.Precision.HIGHEST, preferred_elem...]
    dynamic_update_slice x16 -> x0, local copies, waits for them, and re-layouts: 37.1 us -> none  [on_device(): updates = lax.dynamic_update_slice(updates, current + contribution, corner)]
    all_to_all x0 -> x5, starting transfers between devices: none -> 34.6 us  [the longest x4 29.3 us: spread(): lax.all_to_all(jnp.broadcast_to(chunk[None], (count, *chunk.shape)), axis...]
    pallas_call x0 -> x2, Pallas kernels: none -> 30.6 us  [run_pass(): pl.pallas_call(functools.partial(pass_kernel, modes=modes, size=size, mar...]
    all_to_all x0 -> x5, waiting for transfers between devices: none -> 28.4 us  [the longest x1 20.8 us: total(): lax.all_to_all(sums.reshape(count, -1, LANES), 'col', 0, 0, tiled=True)]
    all_to_all x0 -> x1, blocking collectives: none -> 21 us  [total(): lax.all_to_all(sums.reshape(count, -1, LANES), 'col', 0, 0, tiled=True)]
  transfers between devices with their start and end apart: 18 -> 17, of which waited for: 14 -> 11; matrix products, arithmetic and copies ran while one was open for 2% -> 7% of each run, Pallas kernels for 0% -> 0%
where the time goes in v1:
time: 243 us; the launch traced here: 241 us
  starting transfers between devices  85 us (35%)
  waiting for transfers between devices  75.1 us (31%)
  Pallas kernels  30.6 us (13%)
  blocking collectives  21 us (9%)
  local copies, waits for them, and re-layouts  16.4 us (7%)
  other arithmetic  11.2 us (5%)
    ppermute x6, starting transfers between devices, neighbours(): lax.ppermute(high_strip, axis, up)  38.1 us
    ppermute x6, waiting for transfers between devices, neighbours(): lax.ppermute(low_strip, axis, down)  31.5 us
    pallas_call x2, Pallas kernels, run_pass(): pl.pallas_call(functools.partial(pass_kernel, modes=modes, size=size, mar...  30.6 us
    all_to_all x4, starting transfers between devices, spread(): lax.all_to_all(jnp.broadcast_to(chunk[None], (count, *chunk.shape)), axis...  29.3 us
    all_to_all x1, blocking collectives, total(): lax.all_to_all(sums.reshape(count, -1, LANES), 'col', 0, 0, tiled=True)  21 us
    all_to_all x1, waiting for transfers between devices, total(): lax.all_to_all(sums.reshape(count, -1, LANES), 'col', 0, 0, tiled=True)  20.8 us
    ppermute x6, waiting for transfers between devices, neighbours(): lax.ppermute(high_strip, axis, up)  15.2 us
    ppermute x6, starting transfers between devices, neighbours(): lax.ppermute(low_strip, axis, down)  12.3 us
  transfers between devices with their start and end apart: 17, of which 11 were waited for; matrix products, arithmetic and copies ran while one was open for 7% of the time, Pallas kernels for 0%

profile of v1, /device:TPU:63, one launch (start us, length us, event | category | flops | bytes accessed | tf_op | source)
XLA Modules:
  0.0 241.1 jit_solution(4699726914936697210)
XLA Ops:
  1.6 7.8 %collective-permute-start = (f32[2,64,256]{2,1,0:T(8,128)S(1)}, f32[2,64,256]{2,1,0:T(8,128)S(1)}, u32[]{:S(2)}, u32[]{:S(2)}) collective-permute-start(f32[2,64,256]{2,1,0:T(8,128)S(1)} %get-tuple-element.21), channel_id=1, source_target_pairs={{0,32},{32,64},{64,96},{96,128},{128,160},{160,192},{192,224},{1,3... | collective-permute-start | bytes 393224 | tf_op jit(solution)/shard_map/ppermute | solution.py:147
  9.5 2.1 collective-permute-start.1
  11.6 2.9 %collective-permute-done = f32[2,64,256]{2,1,0:T(8,128)S(1)} collective-permute-done((f32[2,64,256]{2,1,0:T(8,128)S(1)}, f32[2,64,256]{2,1,0:T(8,128)S(1)}, u32[]{:S(2)}, u32[]{:S(2)}) %collective-permute-start) | collective-permute-done | bytes 131104 | tf_op jit(solution)/shard_map/ppermute | solution.py:147
  15.5 9.3 %collective-permute-done.1 = f32[2,64,256]{2,1,0:T(8,128)S(1)} collective-permute-done((f32[2,64,256]{2,1,0:T(8,128)S(1)}, f32[2,64,256]{2,1,0:T(8,128)S(1)}, u32[]{:S(2)}, u32[]{:S(2)}) %collective-permute-start.1) | collective-permute-done | bytes 131104 | tf_op jit(solution)/shard_map/ppermute | solution.py:147
  25.8 3.6 %collective-permute-start.2 = (f32[2,384,128]{2,1,0:T(8,128)}, f32[2,384,128]{2,1,0:T(8,128)S(1)}, u32[]{:S(2)}, u32[]{:S(2)}) collective-permute-start(f32[2,384,128]{2,1,0:T(8,128)} %get-tuple-element.18), channel_id=1, source_target_pairs={{0,1},{1,2},{2,3},{3,4},{4,5},{5,6},{6,7},{7,8},{8,9},{9,10},{10,1... | collective-permute-start | bytes 1179656 | tf_op jit(solution)/shard_map/ppermute | solution.py:147
  29.4 1.9 collective-permute-start.3
  32.3 2.1 collective-permute-done.2
  34.4 6.2 %collective-permute-done.3 = f32[2,384,128]{2,1,0:T(8,128)S(1)} collective-permute-done((f32[2,384,128]{2,1,0:T(8,128)S(1)}, f32[2,384,128]{2,1,0:T(8,128)S(1)}, u32[]{:S(2)}, u32[]{:S(2)}) %collective-permute-start.3) | collective-permute-done | bytes 393248 | tf_op jit(solution)/shard_map/ppermute | solution.py:147
  41.3 15.3 %shard_map.113 = (f32[2,384,512]{2,1,0:T(8,128)S(1)}, f32[9,128,128]{2,1,0:T(8,128)S(1)}) custom-call(s32[8,2]{1,0:T(8,128)S(1)} %copy.18.starts, s32[1]{0:T(128)} %bitcast.12.counts, f32[2,384,512]{2,1,0:T(8,128)S(1)} %pad_maximum_fusion.frame, f32[2,4,128,128]{3,2,1,0:T(8,128)S(1)} %copy-done.1, f32[8,128,128]{2,1,0:T(8,128)S(1)} %convert_multiply_fusion.amplitude, ...), custom_call_target="tpu_custom_call" | custom-call | flops 6442450944 | bytes 6291456 | tf_op jit(solution)/shard_map/pallas_call | solution.py:130
  57.5 5.3 %all-to-all-start = ((f32[32,36,128]{2,1,0:T(8,128)}), f32[32,36,128]{2,1,0:T(8,128)}, u32[]{:S(2)}, u32[]{:S(2)}) async-start(f32[32,36,128]{2,1,0:T(8,128)} %reshape.102), calls=%async_computation | async-start | bytes 1310720 | tf_op jit(solution)/shard_map/all_to_all | solution.py:157
  63.9 2.7 %collective-permute-start.4 = (f32[2,128,512]{2,1,0:T(8,128)}, f32[2,128,512]{2,1,0:T(8,128)}, u32[]{:S(2)}, u32[]{:S(2)}) collective-permute-start(f32[2,128,512]{2,1,0:T(8,128)} %get-tuple-element.14), channel_id=1, source_target_pairs={{0,32},{32,64},{64,96},{96,128},{128,160},{160,192},{192,224},{1,3... | collective-permute-start | bytes 1572872 | tf_op jit(solution)/shard_map/ppermute | solution.py:147
  66.7 2.5 %collective-permute-start.5 = (f32[2,128,512]{2,1,0:T(8,128)}, f32[2,128,512]{2,1,0:T(8,128)}, u32[]{:S(2)}, u32[]{:S(2)}) collective-permute-start(f32[2,128,512]{2,1,0:T(8,128)} %get-tuple-element.15), channel_id=1, source_target_pairs={{32,0},{64,32},{96,64},{128,96},{160,128},{192,160},{224,192},{33,... | collective-permute-start | bytes 1572872 | tf_op jit(solution)/shard_map/ppermute | solution.py:147
  69.2 20.8 %all-to-all-done = f32[32,36,128]{2,1,0:T(8,128)} async-done(((f32[32,36,128]{2,1,0:T(8,128)}), f32[32,36,128]{2,1,0:T(8,128)}, u32[]{:S(2)}, u32[]{:S(2)}) %all-to-all-start) | async-done | bytes 589856 | tf_op jit(solution)/shard_map/all_to_all | solution.py:157
  91.8 3.9 %all-to-all-start.1 = ((f32[8,36,128]{2,1,0:T(8,128)}), f32[8,36,128]{2,1,0:T(8,128)S(1)}, u32[]{:S(2)}, u32[]{:S(2)}) async-start(f32[8,36,128]{2,1,0:T(8,128)} %broadcast_in_dim.22), calls=%async_computation.1 | async-start | bytes 327680 | tf_op jit(solution)/shard_map/all_to_all | solution.py:152
  95.8 7.6 %all-to-all-done.1 = f32[8,36,128]{2,1,0:T(8,128)S(1)} async-done(((f32[8,36,128]{2,1,0:T(8,128)}), f32[8,36,128]{2,1,0:T(8,128)S(1)}, u32[]{:S(2)}, u32[]{:S(2)}) %all-to-all-start.1) | async-done | bytes 147488 | tf_op jit(solution)/shard_map/all_to_all | solution.py:152
  104.3 9.5 %all-to-all-start.2 = ((f32[32,36,128]{2,1,0:T(8,128)}), f32[32,36,128]{2,1,0:T(8,128)}, u32[]{:S(2)}, u32[]{:S(2)}) async-start(f32[32,36,128]{2,1,0:T(8,128)} %broadcast_in_dim.23), calls=%async_computation.2 | async-start | bytes 1310720 | tf_op jit(solution)/shard_map/all_to_all | solution.py:152
  113.8 2.7 %pad_add_fusion = f32[2,384,512]{2,1,0:T(8,128)} fusion(f32[2,128,512]{2,1,0:T(8,128)} %collective-permute-done.5, f32[2,384,512]{2,1,0:T(8,128)S(1)} %get-tuple-element.6, f32[2,128,512]{2,1,0:T(8,128)} %collective-permute-done.4), kind=kLoop, calls=%fused_computation.2 | loop fusion | flops 786432 | bytes 4194304 | tf_op jit(solution)/shard_map/add | solution.py:189
  118.1 3.4 %collective-permute-start.6 = (f32[2,384,128]{2,1,0:T(8,128)S(1)}, f32[2,384,128]{2,1,0:T(8,128)S(1)}, u32[]{:S(2)}, u32[]{:S(2)}) collective-permute-start(f32[2,384,128]{2,1,0:T(8,128)S(1)} %get-tuple-element.12), channel_id=1, source_target_pairs={{0,1},{1,2},{2,3},{3,4},{4,5},{5,6},{6,7},{7,8},{8,9},{9,10},{10,1... | collective-permute-start | bytes 1179656 | tf_op jit(solution)/shard_map/ppermute | solution.py:147
  121.5 1.9 collective-permute-start.7
  123.6 8.9 %collective-permute-done.6 = f32[2,384,128]{2,1,0:T(8,128)S(1)} collective-permute-done((f32[2,384,128]{2,1,0:T(8,128)S(1)}, f32[2,384,128]{2,1,0:T(8,128)S(1)}, u32[]{:S(2)}, u32[]{:S(2)}) %collective-permute-start.6) | collective-permute-done | bytes 393248 | tf_op jit(solution)/shard_map/ppermute | solution.py:147
  134.3 2.4 %select_add_fusion.frame = f32[2,384,512]{2,1,0:T(8,128)S(1)} fusion(f32[2,384,128]{2,1,0:T(8,128)} %collective-permute-done.7, f32[2,384,512]{2,1,0:T(8,128)} %pad_add_fusion, f32[2,384,128]{2,1,0:T(8,128)} %copy-done.12, pred[384,512]{1,0:T(8,128)(4,1)S(1)} %and_and_fusion, f32[2,384,128]{2,1,0:T(8,128)} %copy-done.11, f32[2,384,256]{2,1,0:T(8,128)} %copy-done.8, ...), kind=kLoop, calls=%fused_computation.1 | loop fusion | flops 2359296 | bytes 5701632 | tf_op jit(solution)/shard_map/add | solution.py:198
  138.8 15.3 %shard_map.114 = (f32[2,384,512]{2,1,0:T(8,128)S(1)}, f32[9,128,128]{2,1,0:T(8,128)S(1)}) custom-call(s32[8,2]{1,0:T(8,128)S(1)} %copy.18.starts, s32[1]{0:T(128)} %bitcast.13.counts, f32[2,384,512]{2,1,0:T(8,128)S(1)} %select_add_fusion.frame, f32[2,4,128,128]{3,2,1,0:T(8,128)S(1)} %divide_add_fusion.1.probe, ...), custom_call_target="tpu_custom_call" | custom-call | flops 6442450944 | bytes 6291456 | tf_op jit(solution)/shard_map/pallas_call | solution.py:130
  155.4 21.0 %all_to_all.30 = f32[32,36,128]{2,1,0:T(8,128)} all-to-all(f32[32,36,128]{2,1,0:T(8,128)S(1)} %reshape.105), channel_id=1, replica_groups=mesh['row'=8,'col'=32] {'col'}, dimensions={0} | all-to-all | bytes 1179648 | tf_op jit(solution)/shard_map/all_to_all | solution.py:157
  178.2 7.5 %all-to-all-start.4 = ((f32[8,36,128]{2,1,0:T(8,128)}), f32[8,36,128]{2,1,0:T(8,128)S(1)}, u32[]{:S(2)}, u32[]{:S(2)}) async-start(f32[8,36,128]{2,1,0:T(8,128)} %broadcast_in_dim.40), calls=%async_computation.4 | async-start | bytes 327680 | tf_op jit(solution)/shard_map/all_to_all | solution.py:152
  185.8 1.8 fusion.7
  187.5 7.0 %collective-permute-start.8 = (f32[2,64,512]{2,1,0:T(8,128)}, f32[2,64,512]{2,1,0:T(8,128)S(1)}, u32[]{:S(2)}, u32[]{:S(2)}) collective-permute-start(f32[2,64,512]{2,1,0:T(8,128)} %get-tuple-element.10), channel_id=1, source_target_pairs={{0,32},{32,64},{64,96},{96,128},{128,160},{160,192},{192,224},{1,3... | collective-permute-start | bytes 786440 | tf_op jit(solution)/shard_map/ppermute | solution.py:147
  194.5 1.9 collective-permute-start.9
  197.4 8.3 %all-to-all-start.5 = ((f32[32,36,128]{2,1,0:T(8,128)}), f32[32,36,128]{2,1,0:T(8,128)S(1)}, u32[]{:S(2)}, u32[]{:S(2)}) async-start(f32[32,36,128]{2,1,0:T(8,128)} %broadcast_in_dim.41), calls=%async_computation.5 | async-start | bytes 1310720 | tf_op jit(solution)/shard_map/all_to_all | solution.py:152
  205.7 8.5 %collective-permute-done.9 = f32[2,64,512]{2,1,0:T(8,128)S(1)} collective-permute-done((f32[2,64,512]{2,1,0:T(8,128)S(1)}, f32[2,64,512]{2,1,0:T(8,128)S(1)}, u32[]{:S(2)}, u32[]{:S(2)}) %collective-permute-start.9) | collective-permute-done | bytes 262176 | tf_op jit(solution)/shard_map/ppermute | solution.py:147
  215.8 13.6 %collective-permute-start.10 = (f32[2,256,64]{2,1,0:T(8,128)S(1)}, f32[2,256,64]{2,1,0:T(8,128)S(1)}, u32[]{:S(2)}, u32[]{:S(2)}) collective-permute-start(f32[2,256,64]{2,1,0:T(8,128)S(1)} %get-tuple-element.16), channel_id=1, source_target_pairs={{0,1},{1,2},{2,3},{3,4},{4,5},{5,6},{6,7},{7,8},{8,9},{9,10},{10,1... | collective-permute-start | bytes 393224 | tf_op jit(solution)/shard_map/ppermute | solution.py:147
  229.4 1.9 collective-permute-start.11
  232.7 6.5 %collective-permute-done.11 = f32[2,256,64]{2,1,0:T(8,128)S(1)} collective-permute-done((f32[2,256,64]{2,1,0:T(8,128)S(1)}, f32[2,256,64]{2,1,0:T(8,128)S(1)}, u32[]{:S(2)}, u32[]{:S(2)}) %collective-permute-start.11) | collective-permute-done | bytes 131104 | tf_op jit(solution)/shard_map/ppermute | solution.py:147
  (74 shorter events, 23.1 us)
Async XLA Ops:
  1.6 12.8 %collective-permute-start = (f32[2,64,256]{2,1,0:T(8,128)S(1)}, f32[2,64,256]{2,1,0:T(8,128)S(1)}, u32[]{:S(2)}, u32[]{:S(2)}) collective-permute-start(f32[2,64,256]{2,1,0:T(8,128)S(1)} %get-tuple-element.21), channel_id=1, source_target_pairs={{0,32},{32,64},{64,96},{96,128},{128,160},{160,192},{192,224},{1,3... | collective-permute-start | bytes 393224 | tf_op jit(solution)/shard_map/ppermute | solution.py:147
  9.5 21.8 %copy-start.15 = (s32[1,1,8,2]{2,3,1,0:T(2,128)S(1)}, s32[1,1,8,2]{2,3,1,0:T(2,128)}, u32[]{:S(2)}) copy-start(s32[1,1,8,2]{2,3,1,0:T(2,128)} %param.14) | copy-start | bytes 196
  9.5 22.5 %copy-start.13 = (bf16[1,1,8,128,128]{4,3,2,1,0:T(8,128)(2,1)S(1)}, bf16[1,1,8,128,128]{4,3,2,1,0:T(8,128)(2,1)}, u32[]{:S(2)}) copy-start(bf16[1,1,8,128,128]{4,3,2,1,0:T(8,128)(2,1)} %param.12) | copy-start | bytes 786436
  9.5 22.5 %copy-start.14 = (f32[1,1,8,128]{3,2,1,0:T(8,128)S(1)}, f32[1,1,8,128]{3,2,1,0:T(8,128)}, u32[]{:S(2)}) copy-start(f32[1,1,8,128]{3,2,1,0:T(8,128)} %param.13) | copy-start | bytes 12292
  9.5 15.4 %collective-permute-start.1 = (f32[2,64,256]{2,1,0:T(8,128)S(1)}, f32[2,64,256]{2,1,0:T(8,128)S(1)}, u32[]{:S(2)}, u32[]{:S(2)}) collective-permute-start(f32[2,64,256]{2,1,0:T(8,128)S(1)} %get-tuple-element.20), channel_id=1, source_target_pairs={{32,0},{64,32},{96,64},{128,96},{160,128},{192,160},{224,192},{33,... | collective-permute-start | bytes 393224 | tf_op jit(solution)/shard_map/ppermute | solution.py:147
  24.9 15.8 %copy-start.8 = (f32[2,384,256]{2,1,0:T(8,128)}, f32[2,384,256]{2,1,0:T(8,128)S(1)}, u32[]{:S(2)}) copy-start(f32[2,384,256]{2,1,0:T(8,128)S(1)} %constant_dynamic-update-slice_fusion) | copy-start | bytes 2359300
  25.8 8.6 %collective-permute-start.2 = (f32[2,384,128]{2,1,0:T(8,128)}, f32[2,384,128]{2,1,0:T(8,128)S(1)}, u32[]{:S(2)}, u32[]{:S(2)}) collective-permute-start(f32[2,384,128]{2,1,0:T(8,128)} %get-tuple-element.18), channel_id=1, source_target_pairs={{0,1},{1,2},{2,3},{3,4},{4,5},{5,6},{6,7},{7,8},{8,9},{9,10},{10,1... | collective-permute-start | bytes 1179656 | tf_op jit(solution)/shard_map/ppermute | solution.py:147
  29.4 11.2 %collective-permute-start.3 = (f32[2,384,128]{2,1,0:T(8,128)S(1)}, f32[2,384,128]{2,1,0:T(8,128)S(1)}, u32[]{:S(2)}, u32[]{:S(2)}) collective-permute-start(f32[2,384,128]{2,1,0:T(8,128)S(1)} %get-tuple-element.19), channel_id=1, source_target_pairs={{1,0},{2,1},{3,2},{4,3},{5,4},{6,5},{7,6},{8,7},{9,8},{10,9},{11,1... | collective-permute-start | bytes 1179656 | tf_op jit(solution)/shard_map/ppermute | solution.py:147
  32.2 9.1 %copy-start.1 = (f32[2,4,128,128]{3,2,1,0:T(8,128)S(1)}, f32[2,4,128,128]{3,2,1,0:T(8,128)}, u32[]{:S(2)}) copy-start(f32[2,4,128,128]{3,2,1,0:T(8,128)} %probe.1) | copy-start | bytes 1572868
  32.3 9.1 %copy-start.2 = (bf16[256,256]{1,0:T(8,128)(2,1)S(1)}, bf16[256,256]{1,0:T(8,128)(2,1)}, u32[]{:S(2)}) copy-start(bf16[256,256]{1,0:T(8,128)(2,1)} %constant.34.clone.fh) | copy-start | bytes 393220
  32.3 9.0 %copy-start.3 = (bf16[256,256]{1,0:T(8,128)(2,1)S(1)}, bf16[256,256]{1,0:T(8,128)(2,1)}, u32[]{:S(2)}) copy-start(bf16[256,256]{1,0:T(8,128)(2,1)} %constant.35.clone.fl) | copy-start | bytes 393220
  32.3 9.0 %copy-start.4 = (bf16[256,256]{1,0:T(8,128)(2,1)S(1)}, bf16[256,256]{1,0:T(8,128)(2,1)}, u32[]{:S(2)}) copy-start(bf16[256,256]{1,0:T(8,128)(2,1)} %constant.36.clone.ih) | copy-start | bytes 393220
  32.3 9.0 %copy-start.6 = (bf16[256,256]{1,0:T(8,128)(2,1)S(1)}, bf16[256,256]{1,0:T(8,128)(2,1)}, u32[]{:S(2)}) copy-start(bf16[256,256]{1,0:T(8,128)(2,1)} %constant.37.clone.il) | copy-start | bytes 393220
  34.4 6.4 %copy-start.9 = (f32[2,384,128]{2,1,0:T(8,128)}, f32[2,384,128]{2,1,0:T(8,128)S(1)}, u32[]{:S(2)}) copy-start(f32[2,384,128]{2,1,0:T(8,128)S(1)} %collective-permute-done.2) | copy-start | bytes 1179652
  40.6 0.8 copy-start.11
  57.5 32.5 %all-to-all-start = ((f32[32,36,128]{2,1,0:T(8,128)}), f32[32,36,128]{2,1,0:T(8,128)}, u32[]{:S(2)}, u32[]{:S(2)}) async-start(f32[32,36,128]{2,1,0:T(8,128)} %reshape.102), calls=%async_computation | async-start | bytes 1310720 | tf_op jit(solution)/shard_map/all_to_all | solution.py:157
  63.9 49.8 %collective-permute-start.4 = (f32[2,128,512]{2,1,0:T(8,128)}, f32[2,128,512]{2,1,0:T(8,128)}, u32[]{:S(2)}, u32[]{:S(2)}) collective-permute-start(f32[2,128,512]{2,1,0:T(8,128)} %get-tuple-element.14), channel_id=1, source_target_pairs={{0,32},{32,64},{64,96},{96,128},{128,160},{160,192},{192,224},{1,3... | collective-permute-start | bytes 1572872 | tf_op jit(solution)/shard_map/ppermute | solution.py:147
  66.7 47.1 %collective-permute-start.5 = (f32[2,128,512]{2,1,0:T(8,128)}, f32[2,128,512]{2,1,0:T(8,128)}, u32[]{:S(2)}, u32[]{:S(2)}) collective-permute-start(f32[2,128,512]{2,1,0:T(8,128)} %get-tuple-element.15), channel_id=1, source_target_pairs={{32,0},{64,32},{96,64},{128,96},{160,128},{192,160},{224,192},{33,... | collective-permute-start | bytes 1572872 | tf_op jit(solution)/shard_map/ppermute | solution.py:147
  91.8 11.5 %all-to-all-start.1 = ((f32[8,36,128]{2,1,0:T(8,128)}), f32[8,36,128]{2,1,0:T(8,128)S(1)}, u32[]{:S(2)}, u32[]{:S(2)}) async-start(f32[8,36,128]{2,1,0:T(8,128)} %broadcast_in_dim.22), calls=%async_computation.1 | async-start | bytes 327680 | tf_op jit(solution)/shard_map/all_to_all | solution.py:152
  104.3 32.5 %all-to-all-start.2 = ((f32[32,36,128]{2,1,0:T(8,128)}), f32[32,36,128]{2,1,0:T(8,128)}, u32[]{:S(2)}, u32[]{:S(2)}) async-start(f32[32,36,128]{2,1,0:T(8,128)} %broadcast_in_dim.23), calls=%async_computation.2 | async-start | bytes 1310720 | tf_op jit(solution)/shard_map/all_to_all | solution.py:152
  116.4 17.9 %copy-start.10 = (f32[2,384,128]{2,1,0:T(8,128)S(1)}, f32[2,384,128]{2,1,0:T(8,128)}, u32[]{:S(2)}) copy-start(f32[2,384,128]{2,1,0:T(8,128)} %copy-done.9) | copy-start | bytes 1179652
  118.1 14.4 %collective-permute-start.6 = (f32[2,384,128]{2,1,0:T(8,128)S(1)}, f32[2,384,128]{2,1,0:T(8,128)S(1)}, u32[]{:S(2)}, u32[]{:S(2)}) collective-permute-start(f32[2,384,128]{2,1,0:T(8,128)S(1)} %get-tuple-element.12), channel_id=1, source_target_pairs={{0,1},{1,2},{2,3},{3,4},{4,5},{5,6},{6,7},{7,8},{8,9},{9,10},{10,1... | collective-permute-start | bytes 1179656 | tf_op jit(solution)/shard_map/ppermute | solution.py:147
  121.5 12.8 %collective-permute-start.7 = (f32[2,384,128]{2,1,0:T(8,128)S(1)}, f32[2,384,128]{2,1,0:T(8,128)}, u32[]{:S(2)}, u32[]{:S(2)}) collective-permute-start(f32[2,384,128]{2,1,0:T(8,128)S(1)} %get-tuple-element.13), channel_id=1, source_target_pairs={{1,0},{2,1},{3,2},{4,3},{5,4},{6,5},{7,6},{8,7},{9,8},{10,9},{11,1... | collective-permute-start | bytes 1179656 | tf_op jit(solution)/shard_map/ppermute | solution.py:147
  137.9 0.9 copy-start.5
  137.9 1.0 copy-start.7
  154.1 1.2 copy-start
  178.2 18.2 %all-to-all-start.4 = ((f32[8,36,128]{2,1,0:T(8,128)}), f32[8,36,128]{2,1,0:T(8,128)S(1)}, u32[]{:S(2)}, u32[]{:S(2)}) async-start(f32[8,36,128]{2,1,0:T(8,128)} %broadcast_in_dim.40), calls=%async_computation.4 | async-start | bytes 327680 | tf_op jit(solution)/shard_map/all_to_all | solution.py:152
  187.5 18.2 %collective-permute-start.8 = (f32[2,64,512]{2,1,0:T(8,128)}, f32[2,64,512]{2,1,0:T(8,128)S(1)}, u32[]{:S(2)}, u32[]{:S(2)}) collective-permute-start(f32[2,64,512]{2,1,0:T(8,128)} %get-tuple-element.10), channel_id=1, source_target_pairs={{0,32},{32,64},{64,96},{96,128},{128,160},{160,192},{192,224},{1,3... | collective-permute-start | bytes 786440 | tf_op jit(solution)/shard_map/ppermute | solution.py:147
  194.5 19.7 %collective-permute-start.9 = (f32[2,64,512]{2,1,0:T(8,128)S(1)}, f32[2,64,512]{2,1,0:T(8,128)S(1)}, u32[]{:S(2)}, u32[]{:S(2)}) collective-permute-start(f32[2,64,512]{2,1,0:T(8,128)S(1)} %get-tuple-element.11), channel_id=1, source_target_pairs={{32,0},{64,32},{96,64},{128,96},{160,128},{192,160},{224,192},{33,... | collective-permute-start | bytes 786440 | tf_op jit(solution)/shard_map/ppermute | solution.py:147
  197.4 42.8 %all-to-all-start.5 = ((f32[32,36,128]{2,1,0:T(8,128)}), f32[32,36,128]{2,1,0:T(8,128)S(1)}, u32[]{:S(2)}, u32[]{:S(2)}) async-start(f32[32,36,128]{2,1,0:T(8,128)} %broadcast_in_dim.41), calls=%async_computation.5 | async-start | bytes 1310720 | tf_op jit(solution)/shard_map/all_to_all | solution.py:152
  215.8 16.9 %collective-permute-start.10 = (f32[2,256,64]{2,1,0:T(8,128)S(1)}, f32[2,256,64]{2,1,0:T(8,128)S(1)}, u32[]{:S(2)}, u32[]{:S(2)}) collective-permute-start(f32[2,256,64]{2,1,0:T(8,128)S(1)} %get-tuple-element.16), channel_id=1, source_target_pairs={{0,1},{1,2},{2,3},{3,4},{4,5},{5,6},{6,7},{7,8},{8,9},{9,10},{10,1... | collective-permute-start | bytes 393224 | tf_op jit(solution)/shard_map/ppermute | solution.py:147
  229.4 9.8 %collective-permute-start.11 = (f32[2,256,64]{2,1,0:T(8,128)S(1)}, f32[2,256,64]{2,1,0:T(8,128)S(1)}, u32[]{:S(2)}, u32[]{:S(2)}) collective-permute-start(f32[2,256,64]{2,1,0:T(8,128)S(1)} %get-tuple-element.17), channel_id=1, source_target_pairs={{1,0},{2,1},{3,2},{4,3},{5,4},{6,5},{7,6},{8,7},{9,8},{10,9},{11,1... | collective-permute-start | bytes 393224 | tf_op jit(solution)/shard_map/ppermute | solution.py:147
  (1 other events, 0.7 us)

commit v2 on v1

--- a/solution.py
+++ b/solution.py
@@ -11,6 +11,7 @@
 
 LANES = 128
 SUBLANES = 8
+CORES = 2
 
 
 def dft_tables(length):
@@ -39,9 +40,21 @@
     return mm(lh, rh) + (mm(lh, rl) + mm(ll, rh))
 
 
-def pass_kernel(
-    starts, counts, frame, probe, amplitude, fh, fl, ih, il, updates, sums, *, modes, size, margin
-):
+def pass_kernel(*refs, modes, size, margin, renew):
+    if renew:
+        starts, counts, core, frame, old_probe, mean_mine, mean_other, amplitude, *refs = refs
+        fh, fl, ih, il, updates, mine, other, probe, sums = refs
+        half_rows = mean_mine.shape[0]
+        sums[pl.ds(pl.multiple_of(core[0] * half_rows, size), half_rows)] = mean_mine[...]
+        sums[pl.ds(pl.multiple_of((1 - core[0]) * half_rows, size), half_rows)] = mean_other[...]
+        weight = sums[pl.ds(2 * modes * size, size)]
+        for part in range(2):
+            for m in range(modes):
+                step = sums[pl.ds((part * modes + m) * size, size)] / weight
+                probe[part, m] = old_probe[part, m] + step
+    else:
+        starts, counts, core, frame, probe, amplitude, *refs = refs
+        fh, fl, ih, il, updates, mine, other, sums = refs
     updates[...] = jnp.zeros_like(updates)
     sums[...] = jnp.zeros_like(sums)
     forward = (fh[...], fl[...])
@@ -104,13 +117,13 @@
             pr, pi = probe[0, m], probe[1, m]
             dr = back[m * size : (m + 1) * size, :size] - waves[m][0]
             di = back[m * size : (m + 1) * size, size:] - waves[m][1]
-            sums[m] += patch_re * dr + patch_im * di
-            sums[modes + m] += patch_re * di - patch_im * dr
+            sums[pl.ds(m * size, size)] += patch_re * dr + patch_im * di
+            sums[pl.ds((modes + m) * size, size)] += patch_re * di - patch_im * dr
             add_re = pr * dr + pi * di
             add_im = pr * di - pi * dr
             total_re = add_re if m == 0 else total_re + add_re
             total_im = add_im if m == 0 else total_im + add_im
-        sums[2 * modes] += patch_re * patch_re + patch_im * patch_im
+        sums[pl.ds(2 * modes * size, size)] += patch_re * patch_re + patch_im * patch_im
         updates[0, rows, cols] += placed(total_re)
         updates[1, rows, cols] += placed(total_im)
         return carry
@@ -120,24 +133,32 @@
     for m in range(1, modes):
         strength = strength + probe[0, m] * probe[0, m] + probe[1, m] * probe[1, m]
     updates[...] = updates[...] / jnp.max(strength)
-
-
-def run_pass(starts, count, frame, probe, amplitude, tables, margin):
+    half_rows = mine.shape[0]
+    mine[...] = sums[pl.ds(pl.multiple_of(core[0] * half_rows, size), half_rows)]
+    other[...] = sums[pl.ds(pl.multiple_of((1 - core[0]) * half_rows, size), half_rows)]
+
+
+def run_pass(starts, count, core, frame, probe, means, amplitude, tables, margin):
     modes, size = probe.shape[1], probe.shape[2]
+    renew = means is not None
+    half_rows = (modes + 1) * size
     vmem = pl.BlockSpec(memory_space=pltpu.VMEM)
     smem = pl.BlockSpec(memory_space=pltpu.SMEM)
     flops = 24 * starts.shape[0] * modes * size * (2 * size) ** 2
+    half = jax.ShapeDtypeStruct((half_rows, size), jnp.float32)
+    shapes = [jax.ShapeDtypeStruct(frame.shape, jnp.float32), half, half]
+    if renew:
+        shapes.append(jax.ShapeDtypeStruct(probe.shape, jnp.float32))
+    operands = [frame, probe, *(means or ()), amplitude, *tables]
     return pl.pallas_call(
-        functools.partial(pass_kernel, modes=modes, size=size, margin=margin),
-        out_shape=(
-            jax.ShapeDtypeStruct(frame.shape, jnp.float32),
-            jax.ShapeDtypeStruct((2 * modes + 1, size, size), jnp.float32),
-        ),
-        in_specs=[smem, smem] + [vmem] * 7,
-        out_specs=(vmem, vmem),
+        functools.partial(pass_kernel, modes=modes, size=size, margin=margin, renew=renew),
+        out_shape=shapes,
+        in_specs=[smem] * 3 + [vmem] * len(operands),
+        out_specs=[vmem] * len(shapes),
+        scratch_shapes=[pltpu.VMEM((2 * half_rows, size), jnp.float32)],
         cost_estimate=pl.CostEstimate(flops=flops, bytes_accessed=6 << 20, transcendentals=0),
         compiler_params=pltpu.CompilerParams(vmem_limit_bytes=48 << 20),
-    )(starts, count, frame, probe, amplitude, *tables)
+    )(starts, count, core, *operands)
 
 
 def neighbours(low_strip, high_strip, axis):
@@ -147,16 +168,45 @@
     return lax.ppermute(high_strip, axis, up), lax.ppermute(low_strip, axis, down)
 
 
-def spread(chunk, axis):
-    count = lax.axis_size(axis)
-    return lax.all_to_all(jnp.broadcast_to(chunk[None], (count, *chunk.shape)), axis, 0, 0, tiled=True)
-
-
-def total(sums):
+AXES = ("row", "col")
+
+
+def groups(row_step, col_step):
+    n_row, n_col = lax.axis_size("row"), lax.axis_size("col")
+
+    def flat(zh, x, zl, yc):
+        return (zh * row_step + x) * n_col + zl * col_step + yc
+
+    z = [(zh, zl) for zh in range(n_row // row_step) for zl in range(n_col // col_step)]
+    planes = [
+        [flat(zh, x, zl, y * CORES + c) for x in range(row_step) for y in range(col_step // CORES)]
+        for zh, zl in z
+        for c in range(CORES)
+    ]
+    lines = [[flat(zh, x, zl, yc) for zh, zl in z] for x in range(row_step) for yc in range(col_step)]
+    return planes, lines
+
+
+def exchange(blocks, members):
+    return lax.all_to_all(blocks, AXES, 0, 0, axis_index_groups=members, tiled=True)
+
+
+def spread(chunk, members):
+    return exchange(jnp.broadcast_to(chunk[None], (len(members[0]), *chunk.shape)), members)
+
+
+def swap(block):
     count = lax.axis_size("col")
-    parts = lax.all_to_all(sums.reshape(count, -1, LANES), "col", 0, 0, tiled=True)
-    part = jnp.sum(spread(jnp.sum(parts, axis=0), "row"), axis=0)
-    return spread(part, "col").reshape(sums.shape)
+    return lax.ppermute(block, "col", [(i, i ^ 1) for i in range(count)])
+
+
+def total(mine, other):
+    planes, lines = groups(4, 8)
+    mine = mine + swap(other)
+    parts = exchange(mine.reshape(len(planes[0]), -1, LANES), planes)
+    part = jnp.sum(spread(jnp.sum(parts, axis=0), lines), axis=0)
+    mine = spread(part, planes).reshape(mine.shape)
+    return mine, swap(mine)
 
 
 def at(array, dim, start, stop):
@@ -184,32 +234,38 @@
     low, high = neighbours(at(frame, 2, 0, LANES), at(frame, 2, cols - LANES, cols), "col")
     frame = jnp.concatenate([low, frame, high], axis=2)
 
-    updates, sums = run_pass(starts, count, frame, probe, amplitude, tables, margin)
-    low, high = neighbours(at(updates, 1, 0, 2 * rim), at(updates, 1, rows, tall), "row")
-    updates = updates + padded(low, 1, 0, tall) + padded(high, 1, rows, tall)
-    left = margin, margin + 2 * rim
-    right = margin + cols, margin + cols + 2 * rim
-    low, high = neighbours(at(updates, 2, *left), at(updates, 2, *right), "col")
-    updates = updates + padded(low, 2, margin, wide) + padded(high, 2, margin + cols, wide)
+    core = (lax.axis_index("col") % CORES).reshape(1)
+    left, right = margin, LANES + cols + rim
+    updates, mine, other = run_pass(starts, count, core, frame, probe, None, amplitude, tables, margin)
+    means = total(mine, other)
+    strips = at(updates, 2, left, right)
+    low, high = neighbours(at(strips, 1, 0, 2 * rim), at(strips, 1, rows, tall), "row")
+    strips = strips + padded(low, 1, 0, tall) + padded(high, 1, rows, tall)
+    low, high = neighbours(at(strips, 2, 0, 2 * rim), at(strips, 2, cols, cols + 2 * rim), "col")
+    strips = strips + padded(low, 2, 0, cols + 2 * rim) + padded(high, 2, cols, cols + 2 * rim)
+    updates = padded(strips, 2, left, wide)
     at_row = lax.broadcasted_iota(jnp.int32, (1, tall, 1), 1) + (lax.axis_index("row") * rows - rim)
     at_col = lax.broadcasted_iota(jnp.int32, (1, 1, wide), 2) + (lax.axis_index("col") * cols - LANES)
     inside = (at_row >= 0) & (at_row < rows * lax.axis_size("row"))
     inside = inside & (at_col >= 0) & (at_col < cols * lax.axis_size("col"))
     frame = frame + jnp.where(inside, updates, 0.0)
-    sums = total(sums)
-    probe = probe + sums[: 2 * modes].reshape(probe.shape) / sums[2 * modes]
-
-    updates, sums = run_pass(starts, count, frame, probe, amplitude, tables, margin)
-    low, high = neighbours(at(updates, 1, 0, rim), at(updates, 1, tall - rim, tall), "row")
-    middle = at(updates, 1, rim, rim + rows)
+
+    updates, mine, other, probe = run_pass(
+        starts, count, core, frame, probe, means, amplitude, tables, margin
+    )
+    mine, other = total(mine, other)
+    low, high = neighbours(
+        at(at(updates, 1, 0, rim), 2, left, right), at(at(updates, 1, tall - rim, tall), 2, left, right), "row"
+    )
+    middle = at(at(updates, 1, rim, rim + rows), 2, left, right)
     middle = middle + padded(low, 1, 0, rows) + padded(high, 1, rows - rim, rows)
-    low, high = neighbours(
-        at(middle, 2, margin, LANES), at(middle, 2, LANES + cols, wide - margin), "col"
-    )
-    tile = at(middle, 2, LANES, LANES + cols)
+    low, high = neighbours(at(middle, 2, 0, rim), at(middle, 2, rim + cols, cols + 2 * rim), "col")
+    tile = at(middle, 2, rim, rim + cols)
     tile = tile + padded(low, 2, 0, cols) + padded(high, 2, cols - rim, cols)
     object_out = frame[:, rim : rim + rows, LANES : LANES + cols] + tile
-    sums = total(sums)
+    lower = jnp.where(core[0] == 0, mine, other)
+    upper = jnp.where(core[0] == 0, other, mine)
+    sums = jnp.concatenate([lower, upper]).reshape(-1, size, size)
     probe_out = probe + sums[: 2 * modes].reshape(probe.shape) / sums[2 * modes]
     return object_out, probe_out
 

time: 243 us -> 195 us (0.80)
  blocking collectives: 21 us -> 0 us
  waiting for transfers between devices: 75.1 us -> 57.5 us
  local copies, waits for them, and re-layouts: 16.4 us -> 9.32 us
  Pallas kernels: 30.6 us -> 23.6 us
  starting transfers between devices: 85 us -> 89.9 us
    all_to_all x5 -> x6, waiting for transfers between devices: 28.4 us -> 6.28 us  [exchange(): lax.all_to_all(blocks, AXES, 0, 0, axis_index_groups=members, tiled=True)]
    all_to_all x1 -> x0, blocking collectives: 21 us -> none  [total(): lax.all_to_all(sums.reshape(count, -1, LANES), 'col', 0, 0, tiled=True)]
    ppermute x6, waiting for transfers between devices: 31.5 us -> 41.5 us  [neighbours(): lax.ppermute(low_strip, axis, down)]
    all_to_all x5 -> x6, starting transfers between devices: 34.6 us -> 44.3 us  [exchange(): lax.all_to_all(blocks, AXES, 0, 0, axis_index_groups=members, tiled=True)]
    ppermute x6, waiting for transfers between devices: 15.2 us -> 6.66 us  [neighbours(): lax.ppermute(high_strip, axis, up)]
    pallas_call x2, Pallas kernels: 30.6 us -> 23.6 us  [run_pass(): pl.pallas_call(functools.partial(pass_kernel, modes=modes, size=size, mar...]
    ppermute x6, starting transfers between devices: 38.1 us -> 31.5 us  [neighbours(): lax.ppermute(high_strip, axis, up)]
    ppermute x0 -> x4, waiting for transfers between devices: none -> 3.07 us  [swap(): return lax.ppermute(block, 'col', [(i, i ^ 1) for i in range(count)])]
  transfers between devices with their start and end apart: 17 -> 22, of which waited for: 11 -> 13; matrix products, arithmetic and copies ran while one was open for 7% -> 8% of each run, Pallas kernels for 0% -> 0%
where the time goes in v2:
time: 195 us; the launch traced here: 194 us
  starting transfers between devices  89.9 us (46%)
  waiting for transfers between devices  57.5 us (29%)
  Pallas kernels  23.6 us (12%)
  other arithmetic  11.6 us (6%)
  local copies, waits for them, and re-layouts  9.32 us (5%)
    all_to_all x6, starting transfers between devices, exchange(): lax.all_to_all(blocks, AXES, 0, 0, axis_index_groups=members, tiled=True)  44.3 us
    ppermute x6, waiting for transfers between devices, neighbours(): lax.ppermute(low_strip, axis, down)  41.5 us
    ppermute x6, starting transfers between devices, neighbours(): lax.ppermute(high_strip, axis, up)  31.5 us
    pallas_call x2, Pallas kernels, run_pass(): pl.pallas_call(functools.partial(pass_kernel, modes=modes, size=size, mar...  23.6 us
    ppermute x6, starting transfers between devices, neighbours(): lax.ppermute(low_strip, axis, down)  13.1 us
    ppermute x6, waiting for transfers between devices, neighbours(): lax.ppermute(high_strip, axis, up)  6.66 us
    all_to_all x6, waiting for transfers between devices, exchange(): lax.all_to_all(blocks, AXES, 0, 0, axis_index_groups=members, tiled=True)  6.28 us
    slice x6, local copies, waits for them, and re-layouts, at(): return lax.slice_in_dim(array, start, stop, axis=dim)  4.62 us
  transfers between devices with their start and end apart: 22, of which 13 were waited for; matrix products, arithmetic and copies ran while one was open for 8% of the time, Pallas kernels for 0%

profile of v2, /device:TPU:63, one launch (start us, length us, event | category | flops | bytes accessed | tf_op | source)
XLA Modules:
  0.0 193.8 jit_solution(6457902231353240729)
XLA Ops:
  1.6 7.8 %collective-permute-start = (f32[2,64,256]{2,1,0:T(8,128)S(1)}, f32[2,64,256]{2,1,0:T(8,128)S(1)}, u32[]{:S(2)}, u32[]{:S(2)}) collective-permute-start(f32[2,64,256]{2,1,0:T(8,128)S(1)} %get-tuple-element.29), channel_id=1, source_target_pairs={{0,32},{32,64},{64,96},{96,128},{128,160},{160,192},{192,224},{1,3... | collective-permute-start | bytes 393224 | tf_op jit(solution)/shard_map/ppermute | solution.py:168
  9.5 2.1 %collective-permute-start.1 = (f32[2,64,256]{2,1,0:T(8,128)S(1)}, f32[2,64,256]{2,1,0:T(8,128)S(1)}, u32[]{:S(2)}, u32[]{:S(2)}) collective-permute-start(f32[2,64,256]{2,1,0:T(8,128)S(1)} %get-tuple-element.28), channel_id=1, source_target_pairs={{32,0},{64,32},{96,64},{128,96},{160,128},{192,160},{224,192},{33,... | collective-permute-start | bytes 393224 | tf_op jit(solution)/shard_map/ppermute | solution.py:168
  11.6 2.9 %collective-permute-done = f32[2,64,256]{2,1,0:T(8,128)S(1)} collective-permute-done((f32[2,64,256]{2,1,0:T(8,128)S(1)}, f32[2,64,256]{2,1,0:T(8,128)S(1)}, u32[]{:S(2)}, u32[]{:S(2)}) %collective-permute-start) | collective-permute-done | bytes 131104 | tf_op jit(solution)/shard_map/ppermute | solution.py:168
  15.5 9.3 %collective-permute-done.1 = f32[2,64,256]{2,1,0:T(8,128)S(1)} collective-permute-done((f32[2,64,256]{2,1,0:T(8,128)S(1)}, f32[2,64,256]{2,1,0:T(8,128)S(1)}, u32[]{:S(2)}, u32[]{:S(2)}) %collective-permute-start.1) | collective-permute-done | bytes 131104 | tf_op jit(solution)/shard_map/ppermute | solution.py:168
  24.9 3.6 %collective-permute-start.2 = (f32[2,384,128]{2,1,0:T(8,128)S(1)}, f32[2,384,128]{2,1,0:T(8,128)S(1)}, u32[]{:S(2)}, u32[]{:S(2)}) collective-permute-start(f32[2,384,128]{2,1,0:T(8,128)S(1)} %get-tuple-element.24), channel_id=1, source_target_pairs={{0,1},{1,2},{2,3},{3,4},{4,5},{5,6},{6,7},{7,8},{8,9},{9,10},{10,1... | collective-permute-start | bytes 1179656 | tf_op jit(solution)/shard_map/ppermute | solution.py:168
  28.5 1.9 collective-permute-start.3
  31.5 1.7 collective-permute-done.2
  33.3 6.5 %collective-permute-done.3 = f32[2,384,128]{2,1,0:T(8,128)S(1)} collective-permute-done((f32[2,384,128]{2,1,0:T(8,128)S(1)}, f32[2,384,128]{2,1,0:T(8,128)S(1)}, u32[]{:S(2)}, u32[]{:S(2)}) %collective-permute-start.3) | collective-permute-done | bytes 393248 | tf_op jit(solution)/shard_map/ppermute | solution.py:168
  40.5 11.3 %shard_map.113 = (f32[2,384,512]{2,1,0:T(8,128)S(1)}, f32[640,128]{1,0:T(8,128)S(1)}, f32[640,128]{1,0:T(8,128)S(1)}) custom-call(s32[8,2]{1,0:T(8,128)S(1)} %copy.14.refs_0_, s32[1]{0:T(128)} %bitcast.14.refs_1_, s32[1]{0:T(128)} %bitcast.2.refs_2_, f32[2,384,512]{2,1,0:T(8,128)S(1)} %pad_maximum_fusion.refs_3_, f32[2,4,128,128]{3,2,1,0:T(8,128)S(1)} %copy-done, ...), custom_call_target="tpu_custom_call" | custom-call | flops 6442450944 | bytes 6291456 | tf_op jit(solution)/shard_map/pallas_call | solution.py:153
  53.0 1.9 collective-permute-start.4
  55.0 3.4 %collective-permute-start.5 = (f32[2,128,384]{2,1,0:T(8,128)}, f32[2,128,384]{2,1,0:T(8,128)}, u32[]{:S(2)}, u32[]{:S(2)}) collective-permute-start(f32[2,128,384]{2,1,0:T(8,128)} %get-tuple-element.19), channel_id=1, source_target_pairs={{32,0},{64,32},{96,64},{128,96},{160,128},{192,160},{224,192},{33,... | collective-permute-start | bytes 1179656 | tf_op jit(solution)/shard_map/ppermute | solution.py:168
  60.8 10.9 %all-to-all-start = ((f32[16,40,128]{2,1,0:T(8,128)}), f32[16,40,128]{2,1,0:T(8,128)S(1)}, u32[]{:S(2)}, u32[]{:S(2)}) async-start(f32[16,40,128]{2,1,0:T(8,128)} %bitcast.5), calls=%async_computation | async-start | bytes 655360 | tf_op jit(solution)/shard_map/all_to_all | solution.py:191
  71.8 9.0 %collective-permute-done.5 = f32[2,128,384]{2,1,0:T(8,128)} collective-permute-done((f32[2,128,384]{2,1,0:T(8,128)}, f32[2,128,384]{2,1,0:T(8,128)}, u32[]{:S(2)}, u32[]{:S(2)}) %collective-permute-start.5) | collective-permute-done | bytes 393248 | tf_op jit(solution)/shard_map/ppermute | solution.py:168
  80.8 2.4 %pad_add_fusion.1 = f32[2,384,384]{2,1,0:T(8,128)} fusion(f32[2,128,384]{2,1,0:T(8,128)} %collective-permute-done.5, f32[2,128,384]{2,1,0:T(8,128)S(1)} %collective-permute-done.4, f32[2,384,512]{2,1,0:T(8,128)S(1)} %get-tuple-element.9), kind=kLoop, calls=%fused_computation.3 | loop fusion | flops 589824 | bytes 3145728 | tf_op jit(solution)/shard_map/add | solution.py:243
  84.7 3.3 %all-to-all-start.1 = ((f32[8,40,128]{2,1,0:T(8,128)}), f32[8,40,128]{2,1,0:T(8,128)S(1)}, u32[]{:S(2)}, u32[]{:S(2)}) async-start(f32[8,40,128]{2,1,0:T(8,128)} %broadcast_in_dim.22), calls=%async_computation.1 | async-start | bytes 327680 | tf_op jit(solution)/shard_map/all_to_all | solution.py:191
  88.1 2.1 %fusion.9 = (f32[2,384,128]{2,1,0:T(8,128)}, f32[2,384,128]{2,1,0:T(8,128)}) fusion(f32[2,384,384]{2,1,0:T(8,128)} %pad_add_fusion.1), kind=kLoop, calls=%fused_computation.26 | loop fusion | bytes 1572864 | tf_op jit(solution)/shard_map/slice | solution.py:213
  90.2 6.3 %collective-permute-start.6 = (f32[2,384,128]{2,1,0:T(8,128)}, f32[2,384,128]{2,1,0:T(8,128)}, u32[]{:S(2)}, u32[]{:S(2)}) collective-permute-start(f32[2,384,128]{2,1,0:T(8,128)} %get-tuple-element.20), channel_id=1, source_target_pairs={{0,1},{1,2},{2,3},{3,4},{4,5},{5,6},{6,7},{7,8},{8,9},{9,10},{10,1... | collective-permute-start | bytes 1179656 | tf_op jit(solution)/shard_map/ppermute | solution.py:168
  96.6 1.9 collective-permute-start.7
  99.3 6.1 %all-to-all-start.2 = ((f32[16,40,128]{2,1,0:T(8,128)}), f32[16,40,128]{2,1,0:T(8,128)S(1)}, u32[]{:S(2)}, u32[]{:S(2)}) async-start(f32[16,40,128]{2,1,0:T(8,128)} %broadcast_in_dim.23), calls=%async_computation.2 | async-start | bytes 655360 | tf_op jit(solution)/shard_map/all_to_all | solution.py:191
  106.3 5.4 %all-to-all-done.2 = f32[16,40,128]{2,1,0:T(8,128)S(1)} async-done(((f32[16,40,128]{2,1,0:T(8,128)}), f32[16,40,128]{2,1,0:T(8,128)S(1)}, u32[]{:S(2)}, u32[]{:S(2)}) %all-to-all-start.2) | async-done | bytes 327712 | tf_op jit(solution)/shard_map/all_to_all | solution.py:191
  113.6 1.7 select_add_fusion.refs_3_
  115.4 12.2 %shard_map.114 = (f32[2,384,512]{2,1,0:T(8,128)S(1)}, f32[640,128]{1,0:T(8,128)S(1)}, f32[640,128]{1,0:T(8,128)S(1)}, f32[2,4,128,128]{3,2,1,0:T(8,128)S(1)}) custom-call(s32[8,2]{1,0:T(8,128)S(1)} %copy.14.refs_0_, s32[1]{0:T(128)} %bitcast.15.refs_1_, s32[1]{0:T(128)} %bitcast.2.refs_2_, f32[2,384,512]{2,1,0:T(8,128)} %select_add_fusion.refs_3_, ...), custom_call_target="tpu_custom_call" | custom-call | flops 6442450944 | bytes 6291456 | tf_op jit(solution)/shard_map/pallas_call | solution.py:153
  130.1 12.5 %all-to-all-start.3 = ((f32[16,40,128]{2,1,0:T(8,128)}), f32[16,40,128]{2,1,0:T(8,128)S(1)}, u32[]{:S(2)}, u32[]{:S(2)}) async-start(f32[16,40,128]{2,1,0:T(8,128)} %bitcast.7), calls=%async_computation.3 | async-start | bytes 655360 | tf_op jit(solution)/shard_map/all_to_all | solution.py:191
  142.7 5.1 %collective-permute-start.10 = (f32[2,64,384]{2,1,0:T(8,128)S(1)}, f32[2,64,384]{2,1,0:T(8,128)S(1)}, u32[]{:S(2)}, u32[]{:S(2)}) collective-permute-start(f32[2,64,384]{2,1,0:T(8,128)S(1)} %get-tuple-element.16), channel_id=1, source_target_pairs={{0,32},{32,64},{64,96},{96,128},{128,160},{160,192},{192,224},{1,3... | collective-permute-start | bytes 589832 | tf_op jit(solution)/shard_map/ppermute | solution.py:168
  147.9 1.9 collective-permute-start.11
  150.5 4.5 %all-to-all-start.4 = ((f32[8,40,128]{2,1,0:T(8,128)}), f32[8,40,128]{2,1,0:T(8,128)S(1)}, u32[]{:S(2)}, u32[]{:S(2)}) async-start(f32[8,40,128]{2,1,0:T(8,128)} %broadcast_in_dim.40), calls=%async_computation.4 | async-start | bytes 327680 | tf_op jit(solution)/shard_map/all_to_all | solution.py:191
  155.9 10.1 %collective-permute-done.11 = f32[2,64,384]{2,1,0:T(8,128)S(1)} collective-permute-done((f32[2,64,384]{2,1,0:T(8,128)S(1)}, f32[2,64,384]{2,1,0:T(8,128)S(1)}, u32[]{:S(2)}, u32[]{:S(2)}) %collective-permute-start.11) | collective-permute-done | bytes 196640 | tf_op jit(solution)/shard_map/ppermute | solution.py:168
  167.1 7.0 %all-to-all-start.5 = ((f32[16,40,128]{2,1,0:T(8,128)}), f32[16,40,128]{2,1,0:T(8,128)S(1)}, u32[]{:S(2)}, u32[]{:S(2)}) async-start(f32[16,40,128]{2,1,0:T(8,128)} %broadcast_in_dim.41), calls=%async_computation.5 | async-start | bytes 655360 | tf_op jit(solution)/shard_map/all_to_all | solution.py:191
  174.2 6.7 %collective-permute-start.12 = (f32[2,256,64]{2,1,0:T(8,128)S(1)}, f32[2,256,64]{2,1,0:T(8,128)S(1)}, u32[]{:S(2)}, u32[]{:S(2)}) collective-permute-start(f32[2,256,64]{2,1,0:T(8,128)S(1)} %get-tuple-element.22), channel_id=1, source_target_pairs={{0,1},{1,2},{2,3},{3,4},{4,5},{5,6},{6,7},{7,8},{8,9},{9,10},{10,1... | collective-permute-start | bytes 393224 | tf_op jit(solution)/shard_map/ppermute | solution.py:168
  180.8 1.9 collective-permute-start.13
  184.1 6.5 %collective-permute-done.13 = f32[2,256,64]{2,1,0:T(8,128)S(1)} collective-permute-done((f32[2,256,64]{2,1,0:T(8,128)S(1)}, f32[2,256,64]{2,1,0:T(8,128)S(1)}, u32[]{:S(2)}, u32[]{:S(2)}) %collective-permute-start.13) | collective-permute-done | bytes 131104 | tf_op jit(solution)/shard_map/ppermute | solution.py:168
  190.6 2.1 %fusion.1 = f32[2,256,256]{2,1,0:T(8,128)} fusion(f32[2,256,384]{2,1,0:T(8,128)S(1)} %pad_add_fusion.2, f32[2,384,512]{2,1,0:T(8,128)} %select_add_fusion.refs_3_, f32[2,256,64]{2,1,0:T(8,128)S(1)} %collective-permute-done.13, f32[2,256,64]{2,1,0:T(8,128)S(1)} %collective-permute-done.12), kind=kLoop, calls=%fused_computation.9 | loop fusion | flops 393216 | bytes 1835008 | tf_op jit(solution)/shard_map/add | solution.py:265
  (88 shorter events, 19.6 us)
Async XLA Ops:
  1.6 12.8 %collective-permute-start = (f32[2,64,256]{2,1,0:T(8,128)S(1)}, f32[2,64,256]{2,1,0:T(8,128)S(1)}, u32[]{:S(2)}, u32[]{:S(2)}) collective-permute-start(f32[2,64,256]{2,1,0:T(8,128)S(1)} %get-tuple-element.29), channel_id=1, source_target_pairs={{0,32},{32,64},{64,96},{96,128},{128,160},{160,192},{192,224},{1,3... | collective-permute-start | bytes 393224 | tf_op jit(solution)/shard_map/ppermute | solution.py:168
  9.5 21.0 %copy-start.19 = (s32[1,1,8,2]{2,3,1,0:T(2,128)S(1)}, s32[1,1,8,2]{2,3,1,0:T(2,128)}, u32[]{:S(2)}) copy-start(s32[1,1,8,2]{2,3,1,0:T(2,128)} %param.14) | copy-start | bytes 196
  9.5 21.8 %copy-start.17 = (bf16[1,1,8,128,128]{4,3,2,1,0:T(8,128)(2,1)S(1)}, bf16[1,1,8,128,128]{4,3,2,1,0:T(8,128)(2,1)}, u32[]{:S(2)}) copy-start(bf16[1,1,8,128,128]{4,3,2,1,0:T(8,128)(2,1)} %param.12) | copy-start | bytes 786436
  9.5 21.8 %copy-start.18 = (f32[1,1,8,128]{3,2,1,0:T(8,128)S(1)}, f32[1,1,8,128]{3,2,1,0:T(8,128)}, u32[]{:S(2)}) copy-start(f32[1,1,8,128]{3,2,1,0:T(8,128)} %param.13) | copy-start | bytes 12292
  9.5 15.4 %collective-permute-start.1 = (f32[2,64,256]{2,1,0:T(8,128)S(1)}, f32[2,64,256]{2,1,0:T(8,128)S(1)}, u32[]{:S(2)}, u32[]{:S(2)}) collective-permute-start(f32[2,64,256]{2,1,0:T(8,128)S(1)} %get-tuple-element.28), channel_id=1, source_target_pairs={{32,0},{64,32},{96,64},{128,96},{160,128},{192,160},{224,192},{33,... | collective-permute-start | bytes 393224 | tf_op jit(solution)/shard_map/ppermute | solution.py:168
  24.9 15.1 %copy-start.10 = (f32[2,384,256]{2,1,0:T(8,128)}, f32[2,384,256]{2,1,0:T(8,128)S(1)}, u32[]{:S(2)}) copy-start(f32[2,384,256]{2,1,0:T(8,128)S(1)} %constant_dynamic-update-slice_fusion) | copy-start | bytes 2359300
  24.9 8.3 %collective-permute-start.2 = (f32[2,384,128]{2,1,0:T(8,128)S(1)}, f32[2,384,128]{2,1,0:T(8,128)S(1)}, u32[]{:S(2)}, u32[]{:S(2)}) collective-permute-start(f32[2,384,128]{2,1,0:T(8,128)S(1)} %get-tuple-element.24), channel_id=1, source_target_pairs={{0,1},{1,2},{2,3},{3,4},{4,5},{5,6},{6,7},{7,8},{8,9},{9,10},{10,1... | collective-permute-start | bytes 1179656 | tf_op jit(solution)/shard_map/ppermute | solution.py:168
  28.5 11.2 %collective-permute-start.3 = (f32[2,384,128]{2,1,0:T(8,128)S(1)}, f32[2,384,128]{2,1,0:T(8,128)S(1)}, u32[]{:S(2)}, u32[]{:S(2)}) collective-permute-start(f32[2,384,128]{2,1,0:T(8,128)S(1)} %get-tuple-element.25), channel_id=1, source_target_pairs={{1,0},{2,1},{3,2},{4,3},{5,4},{6,5},{7,6},{8,7},{9,8},{10,9},{11,1... | collective-permute-start | bytes 1179656 | tf_op jit(solution)/shard_map/ppermute | solution.py:168
  31.5 9.1 %copy-start = (f32[2,4,128,128]{3,2,1,0:T(8,128)S(1)}, f32[2,4,128,128]{3,2,1,0:T(8,128)}, u32[]{:S(2)}) copy-start(f32[2,4,128,128]{3,2,1,0:T(8,128)} %refs_4_.3) | copy-start | bytes 1572868
  31.5 9.0 %copy-start.1 = (bf16[256,256]{1,0:T(8,128)(2,1)S(1)}, bf16[256,256]{1,0:T(8,128)(2,1)}, u32[]{:S(2)}) copy-start(bf16[256,256]{1,0:T(8,128)(2,1)} %constant.47.clone.refs_6_.refs_8_) | copy-start | bytes 393220
  31.5 9.0 %copy-start.3 = (bf16[256,256]{1,0:T(8,128)(2,1)S(1)}, bf16[256,256]{1,0:T(8,128)(2,1)}, u32[]{:S(2)}) copy-start(bf16[256,256]{1,0:T(8,128)(2,1)} %constant.48.clone.refs_7_.refs_9_) | copy-start | bytes 393220
  31.5 9.0 %copy-start.5 = (bf16[256,256]{1,0:T(8,128)(2,1)S(1)}, bf16[256,256]{1,0:T(8,128)(2,1)}, u32[]{:S(2)}) copy-start(bf16[256,256]{1,0:T(8,128)(2,1)} %constant.49.clone.refs_8_.refs_10_) | copy-start | bytes 393220
  31.5 9.0 %copy-start.7 = (bf16[256,256]{1,0:T(8,128)(2,1)S(1)}, bf16[256,256]{1,0:T(8,128)(2,1)}, u32[]{:S(2)}) copy-start(bf16[256,256]{1,0:T(8,128)(2,1)} %constant.50.clone.refs_9_.refs_11_) | copy-start | bytes 393220
  53.0 18.7 %collective-permute-start.4 = (f32[2,128,384]{2,1,0:T(8,128)}, f32[2,128,384]{2,1,0:T(8,128)S(1)}, u32[]{:S(2)}, u32[]{:S(2)}) collective-permute-start(f32[2,128,384]{2,1,0:T(8,128)} %get-tuple-element.18), channel_id=1, source_target_pairs={{0,32},{32,64},{64,96},{96,128},{128,160},{160,192},{192,224},{1,3... | collective-permute-start | bytes 1179656 | tf_op jit(solution)/shard_map/ppermute | solution.py:168
  55.0 25.8 %collective-permute-start.5 = (f32[2,128,384]{2,1,0:T(8,128)}, f32[2,128,384]{2,1,0:T(8,128)}, u32[]{:S(2)}, u32[]{:S(2)}) collective-permute-start(f32[2,128,384]{2,1,0:T(8,128)} %get-tuple-element.19), channel_id=1, source_target_pairs={{32,0},{64,32},{96,64},{128,96},{160,128},{192,160},{224,192},{33,... | collective-permute-start | bytes 1179656 | tf_op jit(solution)/shard_map/ppermute | solution.py:168
  58.3 1.7 collective-permute-start.8
  60.8 23.2 %all-to-all-start = ((f32[16,40,128]{2,1,0:T(8,128)}), f32[16,40,128]{2,1,0:T(8,128)S(1)}, u32[]{:S(2)}, u32[]{:S(2)}) async-start(f32[16,40,128]{2,1,0:T(8,128)} %bitcast.5), calls=%async_computation | async-start | bytes 655360 | tf_op jit(solution)/shard_map/all_to_all | solution.py:191
  84.7 13.8 %all-to-all-start.1 = ((f32[8,40,128]{2,1,0:T(8,128)}), f32[8,40,128]{2,1,0:T(8,128)S(1)}, u32[]{:S(2)}, u32[]{:S(2)}) async-start(f32[8,40,128]{2,1,0:T(8,128)} %broadcast_in_dim.22), calls=%async_computation.1 | async-start | bytes 327680 | tf_op jit(solution)/shard_map/all_to_all | solution.py:191
  88.1 24.2 %copy-start.9 = (f32[2,384,384]{2,1,0:T(8,128)S(1)}, f32[2,384,384]{2,1,0:T(8,128)}, u32[]{:S(2)}) copy-start(f32[2,384,384]{2,1,0:T(8,128)} %pad_add_fusion.1) | copy-start | bytes 3538948
  90.2 22.0 %collective-permute-start.6 = (f32[2,384,128]{2,1,0:T(8,128)}, f32[2,384,128]{2,1,0:T(8,128)}, u32[]{:S(2)}, u32[]{:S(2)}) collective-permute-start(f32[2,384,128]{2,1,0:T(8,128)} %get-tuple-element.20), channel_id=1, source_target_pairs={{0,1},{1,2},{2,3},{3,4},{4,5},{5,6},{6,7},{7,8},{8,9},{9,10},{10,1... | collective-permute-start | bytes 1179656 | tf_op jit(solution)/shard_map/ppermute | solution.py:168
  96.6 15.7 %collective-permute-start.7 = (f32[2,384,128]{2,1,0:T(8,128)}, f32[2,384,128]{2,1,0:T(8,128)}, u32[]{:S(2)}, u32[]{:S(2)}) collective-permute-start(f32[2,384,128]{2,1,0:T(8,128)} %get-tuple-element.21), channel_id=1, source_target_pairs={{1,0},{2,1},{3,2},{4,3},{5,4},{6,5},{7,6},{8,7},{9,8},{10,9},{11,1... | collective-permute-start | bytes 1179656 | tf_op jit(solution)/shard_map/ppermute | solution.py:168
  99.3 12.4 %all-to-all-start.2 = ((f32[16,40,128]{2,1,0:T(8,128)}), f32[16,40,128]{2,1,0:T(8,128)S(1)}, u32[]{:S(2)}, u32[]{:S(2)}) async-start(f32[16,40,128]{2,1,0:T(8,128)} %broadcast_in_dim.23), calls=%async_computation.2 | async-start | bytes 655360 | tf_op jit(solution)/shard_map/all_to_all | solution.py:191
  111.7 3.6 %collective-permute-start.9 = (f32[640,128]{1,0:T(8,128)S(1)}, f32[640,128]{1,0:T(8,128)S(1)}, u32[]{:S(2)}, u32[]{:S(2)}) collective-permute-start(f32[640,128]{1,0:T(8,128)S(1)} %bitcast.16), channel_id=1, source_target_pairs={{0,1},{1,0},{2,3},{3,2},{4,5},{5,4},{6,7},{7,6},{8,9},{9,8},{10,11... | collective-permute-start | bytes 983048 | tf_op jit(solution)/shard_map/ppermute | solution.py:200
  127.6 1.7 collective-permute-start.14
  130.1 19.7 %all-to-all-start.3 = ((f32[16,40,128]{2,1,0:T(8,128)}), f32[16,40,128]{2,1,0:T(8,128)S(1)}, u32[]{:S(2)}, u32[]{:S(2)}) async-start(f32[16,40,128]{2,1,0:T(8,128)} %bitcast.7), calls=%async_computation.3 | async-start | bytes 655360 | tf_op jit(solution)/shard_map/all_to_all | solution.py:191
  142.7 13.1 %collective-permute-start.10 = (f32[2,64,384]{2,1,0:T(8,128)S(1)}, f32[2,64,384]{2,1,0:T(8,128)S(1)}, u32[]{:S(2)}, u32[]{:S(2)}) collective-permute-start(f32[2,64,384]{2,1,0:T(8,128)S(1)} %get-tuple-element.16), channel_id=1, source_target_pairs={{0,32},{32,64},{64,96},{96,128},{128,160},{160,192},{192,224},{1,3... | collective-permute-start | bytes 589832 | tf_op jit(solution)/shard_map/ppermute | solution.py:168
  147.9 18.1 %collective-permute-start.11 = (f32[2,64,384]{2,1,0:T(8,128)S(1)}, f32[2,64,384]{2,1,0:T(8,128)S(1)}, u32[]{:S(2)}, u32[]{:S(2)}) collective-permute-start(f32[2,64,384]{2,1,0:T(8,128)S(1)} %get-tuple-element.17), channel_id=1, source_target_pairs={{32,0},{64,32},{96,64},{128,96},{160,128},{192,160},{224,192},{33,... | collective-permute-start | bytes 589832 | tf_op jit(solution)/shard_map/ppermute | solution.py:168
  150.5 15.8 %all-to-all-start.4 = ((f32[8,40,128]{2,1,0:T(8,128)}), f32[8,40,128]{2,1,0:T(8,128)S(1)}, u32[]{:S(2)}, u32[]{:S(2)}) async-start(f32[8,40,128]{2,1,0:T(8,128)} %broadcast_in_dim.40), calls=%async_computation.4 | async-start | bytes 327680 | tf_op jit(solution)/shard_map/all_to_all | solution.py:191
  167.1 15.7 %all-to-all-start.5 = ((f32[16,40,128]{2,1,0:T(8,128)}), f32[16,40,128]{2,1,0:T(8,128)S(1)}, u32[]{:S(2)}, u32[]{:S(2)}) async-start(f32[16,40,128]{2,1,0:T(8,128)} %broadcast_in_dim.41), calls=%async_computation.5 | async-start | bytes 655360 | tf_op jit(solution)/shard_map/all_to_all | solution.py:191
  174.2 10.0 %collective-permute-start.12 = (f32[2,256,64]{2,1,0:T(8,128)S(1)}, f32[2,256,64]{2,1,0:T(8,128)S(1)}, u32[]{:S(2)}, u32[]{:S(2)}) collective-permute-start(f32[2,256,64]{2,1,0:T(8,128)S(1)} %get-tuple-element.22), channel_id=1, source_target_pairs={{0,1},{1,2},{2,3},{3,4},{4,5},{5,6},{6,7},{7,8},{8,9},{9,10},{10,1... | collective-permute-start | bytes 393224 | tf_op jit(solution)/shard_map/ppermute | solution.py:168
  180.8 9.8 %collective-permute-start.13 = (f32[2,256,64]{2,1,0:T(8,128)S(1)}, f32[2,256,64]{2,1,0:T(8,128)S(1)}, u32[]{:S(2)}, u32[]{:S(2)}) collective-permute-start(f32[2,256,64]{2,1,0:T(8,128)S(1)} %get-tuple-element.23), channel_id=1, source_target_pairs={{1,0},{2,1},{3,2},{4,3},{5,4},{6,5},{7,6},{8,7},{9,8},{10,9},{11,1... | collective-permute-start | bytes 393224 | tf_op jit(solution)/shard_map/ppermute | solution.py:168
  182.8 10.0 %collective-permute-start.15 = (f32[640,128]{1,0:T(8,128)S(1)}, f32[640,128]{1,0:T(8,128)S(1)}, u32[]{:S(2)}, u32[]{:S(2)}) collective-permute-start(f32[640,128]{1,0:T(8,128)S(1)} %bitcast.19), channel_id=1, source_target_pairs={{0,1},{1,0},{2,3},{3,2},{4,5},{5,4},{6,7},{7,6},{8,9},{9,8},{10,11... | collective-permute-start | bytes 983048 | tf_op jit(solution)/shard_map/ppermute | solution.py:200
  (10 other events, 21.9 us)

commit v3 on v2

--- a/solution.py
+++ b/solution.py
@@ -8,6 +8,7 @@
 from jax.experimental import pallas as pl
 from jax.experimental.pallas import tpu as pltpu
 from jax.sharding import PartitionSpec as P
+
 
 LANES = 128
 SUBLANES = 8
@@ -163,9 +164,15 @@
 
 def neighbours(low_strip, high_strip, axis):
     count = lax.axis_size(axis)
-    up = [(i, i + 1) for i in range(count - 1)]
-    down = [(i + 1, i) for i in range(count - 1)]
-    return lax.ppermute(high_strip, axis, up), lax.ppermute(low_strip, axis, down)
+    odd = lax.axis_index(axis) % 2 == 1
+
+    def meet(block, start):
+        pairs = [(i, i + 1) for i in range(start, count - 1, 2)]
+        return lax.ppermute(block, axis, pairs + [(j, i) for i, j in pairs])
+
+    first = meet(jnp.where(odd, high_strip, low_strip), 1)
+    second = meet(jnp.where(odd, low_strip, high_strip), 0)
+    return jnp.where(odd, second, first), jnp.where(odd, first, second)
 
 
 AXES = ("row", "col")
@@ -254,10 +261,9 @@
         starts, count, core, frame, probe, means, amplitude, tables, margin
     )
     mine, other = total(mine, other)
-    low, high = neighbours(
-        at(at(updates, 1, 0, rim), 2, left, right), at(at(updates, 1, tall - rim, tall), 2, left, right), "row"
-    )
-    middle = at(at(updates, 1, rim, rim + rows), 2, left, right)
+    strips = at(updates, 2, left, right)
+    low, high = neighbours(at(strips, 1, 0, rim), at(strips, 1, tall - rim, tall), "row")
+    middle = at(strips, 1, rim, rim + rows)
     middle = middle + padded(low, 1, 0, rows) + padded(high, 1, rows - rim, rows)
     low, high = neighbours(at(middle, 2, 0, rim), at(middle, 2, rim + cols, cols + 2 * rim), "col")
     tile = at(middle, 2, rim, rim + cols)

time: 195 us -> 182 us (0.933)
  the two profiles are of different devices: /device:TPU:63 before, /device:TPU:25 now
where the time goes in v3:
time: 182 us; the launch traced here: 181 us
  starting transfers between devices  95.4 us (52%)
  waiting for transfers between devices  39.1 us (21%)
  other arithmetic  20.7 us (11%)
  Pallas kernels  19.5 us (11%)
  local copies, waits for them, and re-layouts  4.41 us (2%)
    all_to_all x6, starting transfers between devices, exchange(): lax.all_to_all(blocks, AXES, 0, 0, axis_index_groups=members, tiled=True)  55.4 us
    ppermute x12, starting transfers between devices, meet(): return lax.ppermute(block, axis, pairs + [(j, i) for i, j in pairs])  32.6 us
    all_to_all x6, waiting for transfers between devices, exchange(): lax.all_to_all(blocks, AXES, 0, 0, axis_index_groups=members, tiled=True)  22.9 us
    pallas_call x2, Pallas kernels, run_pass(): pl.pallas_call(functools.partial(pass_kernel, modes=modes, size=size, mar...  19.5 us
    ppermute x12, waiting for transfers between devices, meet(): return lax.ppermute(block, axis, pairs + [(j, i) for i, j in pairs])  12.8 us
    ppermute x4, starting transfers between devices, swap(): return lax.ppermute(block, 'col', [(i, i ^ 1) for i in range(count)])  7.37 us
    select_n x6, other arithmetic, neighbours(): second = meet(jnp.where(odd, low_strip, high_strip), 0)  4.55 us
  transfers between devices with their start and end apart: 22, of which 11 were waited for; matrix products, arithmetic and copies ran while one was open for 9% of the time, Pallas kernels for 0%

profile of v3, /device:TPU:25, one launch (start us, length us, event | category | flops | bytes accessed | tf_op | source)
XLA Modules:
  0.0 180.9 jit_solution(10214487296711767299)
XLA Ops:
  3.6 2.5 %collective-permute-done = f32[2,64,256]{2,1,0:T(8,128)S(1)} collective-permute-done((f32[2,64,256]{2,1,0:T(8,128)S(1)}, f32[2,64,256]{2,1,0:T(8,128)S(1)}, u32[]{:S(2)}, u32[]{:S(2)}) %collective-permute-start) | collective-permute-done | bytes 131104 | tf_op jit(solution)/shard_map/ppermute | solution.py:171
  7.5 1.6 collective-permute-start.2
  9.1 3.2 %collective-permute-start.3 = (f32[2,384,128]{2,1,0:T(8,128)S(1)}, f32[2,384,128]{2,1,0:T(8,128)S(1)}, u32[]{:S(2)}, u32[]{:S(2)}) collective-permute-start(f32[2,384,128]{2,1,0:T(8,128)S(1)} %get-tuple-element.31), channel_id=1, source_target_pairs={{1,2},{3,4},{5,6},{7,8},{9,10},{11,12},{13,14},{15,16},{17,18},{19... | collective-permute-start | bytes 1179656 | tf_op jit(solution)/shard_map/ppermute | solution.py:171
  13.3 7.0 %collective-permute-done.3 = f32[2,384,128]{2,1,0:T(8,128)S(1)} collective-permute-done((f32[2,384,128]{2,1,0:T(8,128)S(1)}, f32[2,384,128]{2,1,0:T(8,128)S(1)}, u32[]{:S(2)}, u32[]{:S(2)}) %collective-permute-start.3) | collective-permute-done | bytes 393248 | tf_op jit(solution)/shard_map/ppermute | solution.py:171
  21.8 9.3 %shard_map.113 = (f32[2,384,512]{2,1,0:T(8,128)S(1)}, f32[640,128]{1,0:T(8,128)S(1)}, f32[640,128]{1,0:T(8,128)S(1)}) custom-call(s32[8,2]{1,0:T(8,128)S(1)} %copy.14.refs_0_, s32[1]{0:T(128)} %bitcast.14.refs_1_, s32[1]{0:T(128)} %bitcast.2.refs_2_, f32[2,384,512]{2,1,0:T(8,128)S(1)} %pad_maximum_fusion.refs_3_, f32[2,4,128,128]{3,2,1,0:T(8,128)S(1)} %copy-done, ...), custom_call_target="tpu_custom_call" | custom-call | flops 6442450944 | bytes 6291456 | tf_op jit(solution)/shard_map/pallas_call | solution.py:154
  32.3 12.0 %collective-permute-start.4 = (f32[2,128,384]{2,1,0:T(8,128)}, f32[2,128,384]{2,1,0:T(8,128)}, u32[]{:S(2)}, u32[]{:S(2)}) collective-permute-start(f32[2,128,384]{2,1,0:T(8,128)} %get-tuple-element.18), channel_id=1, source_target_pairs={{0,32},{64,96},{128,160},{192,224},{32,0},{96,64},{160,128},{224,1... | collective-permute-start | bytes 1179656 | tf_op jit(solution)/shard_map/ppermute | solution.py:171
  45.7 1.8 collective-permute-done.8
  47.5 1.8 add.107
  49.2 17.1 %all-to-all-start = ((f32[16,40,128]{2,1,0:T(8,128)}), f32[16,40,128]{2,1,0:T(8,128)S(1)}, u32[]{:S(2)}, u32[]{:S(2)}) async-start(f32[16,40,128]{2,1,0:T(8,128)} %bitcast.5), calls=%async_computation | async-start | bytes 655360 | tf_op jit(solution)/shard_map/all_to_all | solution.py:198
  67.5 1.5 pad_add_fusion.1
  69.0 4.0 %all-to-all-done = f32[16,40,128]{2,1,0:T(8,128)S(1)} async-done(((f32[16,40,128]{2,1,0:T(8,128)}), f32[16,40,128]{2,1,0:T(8,128)S(1)}, u32[]{:S(2)}, u32[]{:S(2)}) %all-to-all-start) | async-done | bytes 327712 | tf_op jit(solution)/shard_map/all_to_all | solution.py:198
  73.7 11.0 %all-to-all-start.1 = ((f32[8,40,128]{2,1,0:T(8,128)}), f32[8,40,128]{2,1,0:T(8,128)S(1)}, u32[]{:S(2)}, u32[]{:S(2)}) async-start(f32[8,40,128]{2,1,0:T(8,128)} %broadcast_in_dim.22), calls=%async_computation.1 | async-start | bytes 327680 | tf_op jit(solution)/shard_map/all_to_all | solution.py:198
  84.8 2.0 %slice_select_fusion.1 = (f32[2,384,128]{2,1,0:T(8,128)}, f32[2,384,128]{2,1,0:T(8,128)}) fusion(f32[2,384,384]{2,1,0:T(8,128)} %pad_add_fusion.1, pred[]{:T(512)S(6)} %eq.22), kind=kLoop, calls=%fused_computation.14 | loop fusion | flops 196608 | bytes 1572865 | tf_op jit(solution)/shard_map/jit(_where)/select_n | solution.py:174
  87.5 4.5 %collective-permute-start.7 = (f32[2,384,128]{2,1,0:T(8,128)}, f32[2,384,128]{2,1,0:T(8,128)}, u32[]{:S(2)}, u32[]{:S(2)}) collective-permute-start(f32[2,384,128]{2,1,0:T(8,128)} %get-tuple-element.21), channel_id=1, source_target_pairs={{1,2},{3,4},{5,6},{7,8},{9,10},{11,12},{13,14},{15,16},{17,18},{19... | collective-permute-start | bytes 1179656 | tf_op jit(solution)/shard_map/ppermute | solution.py:171
  94.1 4.2 %all-to-all-start.2 = ((f32[16,40,128]{2,1,0:T(8,128)}), f32[16,40,128]{2,1,0:T(8,128)S(1)}, u32[]{:S(2)}, u32[]{:S(2)}) async-start(f32[16,40,128]{2,1,0:T(8,128)} %broadcast_in_dim.23), calls=%async_computation.2 | async-start | bytes 655360 | tf_op jit(solution)/shard_map/all_to_all | solution.py:198
  99.1 1.9 %broadcast_select_fusion.3 = (f32[2,384,128]{2,1,0:T(8,128)}, f32[2,384,128]{2,1,0:T(8,128)}) fusion(f32[2,384,128]{2,1,0:T(8,128)S(1)} %collective-permute-done.6, f32[2,384,128]{2,1,0:T(8,128)} %collective-permute-done.7, pred[]{:T(512)S(6)} %eq.22), kind=kLoop, calls=%fused_computation.24 | loop fusion | flops 196608 | bytes 1572865 | tf_op jit(solution)/shard_map/jit(_where)/select_n | solution.py:175
  101.0 3.2 %all-to-all-done.2 = f32[16,40,128]{2,1,0:T(8,128)S(1)} async-done(((f32[16,40,128]{2,1,0:T(8,128)}), f32[16,40,128]{2,1,0:T(8,128)S(1)}, u32[]{:S(2)}, u32[]{:S(2)}) %all-to-all-start.2) | async-done | bytes 327712 | tf_op jit(solution)/shard_map/all_to_all | solution.py:198
  104.2 3.4 %collective-permute-start.9 = (f32[640,128]{1,0:T(8,128)S(1)}, f32[640,128]{1,0:T(8,128)S(1)}, u32[]{:S(2)}, u32[]{:S(2)}) collective-permute-start(f32[640,128]{1,0:T(8,128)S(1)} %bitcast.16), channel_id=1, source_target_pairs={{0,1},{1,0},{2,3},{3,2},{4,5},{5,4},{6,7},{7,6},{8,9},{9,8},{10,11... | collective-permute-start | bytes 983048 | tf_op jit(solution)/shard_map/ppermute | solution.py:207
  109.3 1.7 select_add_fusion.refs_3_
  111.0 10.2 %shard_map.114 = (f32[2,384,512]{2,1,0:T(8,128)S(1)}, f32[640,128]{1,0:T(8,128)S(1)}, f32[640,128]{1,0:T(8,128)S(1)}, f32[2,4,128,128]{3,2,1,0:T(8,128)S(1)}) custom-call(s32[8,2]{1,0:T(8,128)S(1)} %copy.14.refs_0_, s32[1]{0:T(128)} %bitcast.15.refs_1_, s32[1]{0:T(128)} %bitcast.2.refs_2_, f32[2,384,512]{2,1,0:T(8,128)} %select_add_fusion.refs_3_, ...), custom_call_target="tpu_custom_call" | custom-call | flops 6442450944 | bytes 6291456 | tf_op jit(solution)/shard_map/pallas_call | solution.py:154
  121.3 1.6 collective-permute-done.14
  123.6 13.5 %all-to-all-start.3 = ((f32[16,40,128]{2,1,0:T(8,128)}), f32[16,40,128]{2,1,0:T(8,128)S(1)}, u32[]{:S(2)}, u32[]{:S(2)}) async-start(f32[16,40,128]{2,1,0:T(8,128)} %bitcast.7), calls=%async_computation.3 | async-start | bytes 655360 | tf_op jit(solution)/shard_map/all_to_all | solution.py:198
  137.4 1.5 collective-permute-start.10
  139.5 4.8 %all-to-all-done.3 = f32[16,40,128]{2,1,0:T(8,128)S(1)} async-done(((f32[16,40,128]{2,1,0:T(8,128)}), f32[16,40,128]{2,1,0:T(8,128)S(1)}, u32[]{:S(2)}, u32[]{:S(2)}) %all-to-all-start.3) | async-done | bytes 327712 | tf_op jit(solution)/shard_map/all_to_all | solution.py:198
  145.0 4.7 %all-to-all-start.4 = ((f32[8,40,128]{2,1,0:T(8,128)}), f32[8,40,128]{2,1,0:T(8,128)S(1)}, u32[]{:S(2)}, u32[]{:S(2)}) async-start(f32[8,40,128]{2,1,0:T(8,128)} %broadcast_in_dim.40), calls=%async_computation.4 | async-start | bytes 327680 | tf_op jit(solution)/shard_map/all_to_all | solution.py:198
  150.0 9.1 %all-to-all-done.4 = f32[8,40,128]{2,1,0:T(8,128)S(1)} async-done(((f32[8,40,128]{2,1,0:T(8,128)}), f32[8,40,128]{2,1,0:T(8,128)S(1)}, u32[]{:S(2)}, u32[]{:S(2)}) %all-to-all-start.4) | async-done | bytes 163872 | tf_op jit(solution)/shard_map/all_to_all | solution.py:198
  159.8 4.9 %all-to-all-start.5 = ((f32[16,40,128]{2,1,0:T(8,128)}), f32[16,40,128]{2,1,0:T(8,128)S(1)}, u32[]{:S(2)}, u32[]{:S(2)}) async-start(f32[16,40,128]{2,1,0:T(8,128)} %broadcast_in_dim.41), calls=%async_computation.5 | async-start | bytes 655360 | tf_op jit(solution)/shard_map/all_to_all | solution.py:198
  164.8 3.1 %collective-permute-start.12 = (f32[2,256,64]{2,1,0:T(8,128)S(1)}, f32[2,256,64]{2,1,0:T(8,128)S(1)}, u32[]{:S(2)}, u32[]{:S(2)}) collective-permute-start(f32[2,256,64]{2,1,0:T(8,128)S(1)} %get-tuple-element.22), channel_id=1, source_target_pairs={{0,1},{2,3},{4,5},{6,7},{8,9},{10,11},{12,13},{14,15},{16,17},{18,... | collective-permute-start | bytes 393224 | tf_op jit(solution)/shard_map/ppermute | solution.py:171
  167.9 1.9 %collective-permute-start.13 = (f32[2,256,64]{2,1,0:T(8,128)S(1)}, f32[2,256,64]{2,1,0:T(8,128)S(1)}, u32[]{:S(2)}, u32[]{:S(2)}) collective-permute-start(f32[2,256,64]{2,1,0:T(8,128)S(1)} %get-tuple-element.23), channel_id=1, source_target_pairs={{1,2},{3,4},{5,6},{7,8},{9,10},{11,12},{13,14},{15,16},{17,18},{19... | collective-permute-start | bytes 393224 | tf_op jit(solution)/shard_map/ppermute | solution.py:171
  170.5 3.9 %collective-permute-start.15 = (f32[640,128]{1,0:T(8,128)S(1)}, f32[640,128]{1,0:T(8,128)S(1)}, u32[]{:S(2)}, u32[]{:S(2)}) collective-permute-start(f32[640,128]{1,0:T(8,128)S(1)} %bitcast.19), channel_id=1, source_target_pairs={{0,1},{1,0},{2,3},{3,2},{4,5},{5,4},{6,7},{7,6},{8,9},{9,8},{10,11... | collective-permute-start | bytes 983048 | tf_op jit(solution)/shard_map/ppermute | solution.py:207
  174.4 3.3 %collective-permute-done.13 = f32[2,256,64]{2,1,0:T(8,128)S(1)} collective-permute-done((f32[2,256,64]{2,1,0:T(8,128)S(1)}, f32[2,256,64]{2,1,0:T(8,128)S(1)}, u32[]{:S(2)}, u32[]{:S(2)}) %collective-permute-start.13) | collective-permute-done | bytes 131104 | tf_op jit(solution)/shard_map/ppermute | solution.py:171
  177.8 2.1 %fusion.1 = f32[2,256,256]{2,1,0:T(8,128)} fusion(f32[2,256,384]{2,1,0:T(8,128)S(1)} %pad_add_fusion.2, f32[2,384,512]{2,1,0:T(8,128)} %select_add_fusion.refs_3_, f32[2,256,64]{2,1,0:T(8,128)S(1)} %get-tuple-element.35, f32[2,256,64]{2,1,0:T(8,128)S(1)} %get-tuple-element.34), kind=kLoop, calls=%fused_computation.10 | loop fusion | flops 393216 | bytes 1835008 | tf_op jit(solution)/shard_map/add | solution.py:271
  (100 shorter events, 20.9 us)
Async XLA Ops:
  1.6 4.5 %collective-permute-start = (f32[2,64,256]{2,1,0:T(8,128)S(1)}, f32[2,64,256]{2,1,0:T(8,128)S(1)}, u32[]{:S(2)}, u32[]{:S(2)}) collective-permute-start(f32[2,64,256]{2,1,0:T(8,128)S(1)} %get-tuple-element.36), channel_id=1, source_target_pairs={{0,32},{64,96},{128,160},{192,224},{32,0},{96,64},{160,128},{224,1... | collective-permute-start | bytes 393224 | tf_op jit(solution)/shard_map/ppermute | solution.py:171
  2.9 3.2 %collective-permute-start.1 = (f32[2,64,256]{2,1,0:T(8,128)S(1)}, f32[2,64,256]{2,1,0:T(8,128)S(1)}, u32[]{:S(2)}, u32[]{:S(2)}) collective-permute-start(f32[2,64,256]{2,1,0:T(8,128)S(1)} %get-tuple-element.37), channel_id=1, source_target_pairs={{32,64},{96,128},{160,192},{64,32},{128,96},{192,160},{33,65},{97,... | collective-permute-start | bytes 393224 | tf_op jit(solution)/shard_map/ppermute | solution.py:171
  6.1 14.2 %copy-start.16 = (f32[2,64,256]{2,1,0:T(8,128)}, f32[2,64,256]{2,1,0:T(8,128)S(1)}, u32[]{:S(2)}) copy-start(f32[2,64,256]{2,1,0:T(8,128)S(1)} %get-tuple-element.40) | copy-start | bytes 393220
  6.2 14.2 %copy-start.18 = (f32[2,64,256]{2,1,0:T(8,128)}, f32[2,64,256]{2,1,0:T(8,128)S(1)}, u32[]{:S(2)}) copy-start(f32[2,64,256]{2,1,0:T(8,128)S(1)} %get-tuple-element.41) | copy-start | bytes 393220
  6.2 6.2 %copy-start.23 = (s32[1,1,8,2]{2,3,1,0:T(2,128)S(1)}, s32[1,1,8,2]{2,3,1,0:T(2,128)}, u32[]{:S(2)}) copy-start(s32[1,1,8,2]{2,3,1,0:T(2,128)} %param.14) | copy-start | bytes 196
  6.2 6.9 %copy-start.21 = (bf16[1,1,8,128,128]{4,3,2,1,0:T(8,128)(2,1)S(1)}, bf16[1,1,8,128,128]{4,3,2,1,0:T(8,128)(2,1)}, u32[]{:S(2)}) copy-start(bf16[1,1,8,128,128]{4,3,2,1,0:T(8,128)(2,1)} %param.12) | copy-start | bytes 786436
  6.2 6.9 %copy-start.22 = (f32[1,1,8,128]{3,2,1,0:T(8,128)S(1)}, f32[1,1,8,128]{3,2,1,0:T(8,128)}, u32[]{:S(2)}) copy-start(f32[1,1,8,128]{3,2,1,0:T(8,128)} %param.13) | copy-start | bytes 12292
  7.5 12.9 %copy-start.10 = (f32[2,256,256]{2,1,0:T(8,128)S(1)}, f32[2,256,256]{2,1,0:T(8,128)}, u32[]{:S(2)}) copy-start(f32[2,256,256]{2,1,0:T(8,128)} %param.10) | copy-start | bytes 1572868
  7.5 5.8 %collective-permute-start.2 = (f32[2,384,128]{2,1,0:T(8,128)S(1)}, f32[2,384,128]{2,1,0:T(8,128)S(1)}, u32[]{:S(2)}, u32[]{:S(2)}) collective-permute-start(f32[2,384,128]{2,1,0:T(8,128)S(1)} %get-tuple-element.30), channel_id=1, source_target_pairs={{0,1},{2,3},{4,5},{6,7},{8,9},{10,11},{12,13},{14,15},{16,17},{18,... | collective-permute-start | bytes 1179656 | tf_op jit(solution)/shard_map/ppermute | solution.py:171
  9.1 11.2 %collective-permute-start.3 = (f32[2,384,128]{2,1,0:T(8,128)S(1)}, f32[2,384,128]{2,1,0:T(8,128)S(1)}, u32[]{:S(2)}, u32[]{:S(2)}) collective-permute-start(f32[2,384,128]{2,1,0:T(8,128)S(1)} %get-tuple-element.31), channel_id=1, source_target_pairs={{1,2},{3,4},{5,6},{7,8},{9,10},{11,12},{13,14},{15,16},{17,18},{19... | collective-permute-start | bytes 1179656 | tf_op jit(solution)/shard_map/ppermute | solution.py:171
  32.3 34.1 %collective-permute-start.4 = (f32[2,128,384]{2,1,0:T(8,128)}, f32[2,128,384]{2,1,0:T(8,128)}, u32[]{:S(2)}, u32[]{:S(2)}) collective-permute-start(f32[2,128,384]{2,1,0:T(8,128)} %get-tuple-element.18), channel_id=1, source_target_pairs={{0,32},{64,96},{128,160},{192,224},{32,0},{96,64},{160,128},{224,1... | collective-permute-start | bytes 1179656 | tf_op jit(solution)/shard_map/ppermute | solution.py:171
  44.3 22.1 %collective-permute-start.5 = (f32[2,128,384]{2,1,0:T(8,128)}, f32[2,128,384]{2,1,0:T(8,128)}, u32[]{:S(2)}, u32[]{:S(2)}) collective-permute-start(f32[2,128,384]{2,1,0:T(8,128)} %get-tuple-element.19), channel_id=1, source_target_pairs={{32,64},{96,128},{160,192},{64,32},{128,96},{192,160},{33,65},{97,... | collective-permute-start | bytes 1179656 | tf_op jit(solution)/shard_map/ppermute | solution.py:171
  45.7 1.8 collective-permute-start.8
  49.2 23.8 %all-to-all-start = ((f32[16,40,128]{2,1,0:T(8,128)}), f32[16,40,128]{2,1,0:T(8,128)S(1)}, u32[]{:S(2)}, u32[]{:S(2)}) async-start(f32[16,40,128]{2,1,0:T(8,128)} %bitcast.5), calls=%async_computation | async-start | bytes 655360 | tf_op jit(solution)/shard_map/all_to_all | solution.py:198
  73.7 19.6 %all-to-all-start.1 = ((f32[8,40,128]{2,1,0:T(8,128)}), f32[8,40,128]{2,1,0:T(8,128)S(1)}, u32[]{:S(2)}, u32[]{:S(2)}) async-start(f32[8,40,128]{2,1,0:T(8,128)} %broadcast_in_dim.22), calls=%async_computation.1 | async-start | bytes 327680 | tf_op jit(solution)/shard_map/all_to_all | solution.py:198
  86.8 20.8 %copy-start.9 = (f32[2,384,384]{2,1,0:T(8,128)S(1)}, f32[2,384,384]{2,1,0:T(8,128)}, u32[]{:S(2)}) copy-start(f32[2,384,384]{2,1,0:T(8,128)} %pad_add_fusion.1) | copy-start | bytes 3538948
  86.8 12.3 %collective-permute-start.6 = (f32[2,384,128]{2,1,0:T(8,128)}, f32[2,384,128]{2,1,0:T(8,128)S(1)}, u32[]{:S(2)}, u32[]{:S(2)}) collective-permute-start(f32[2,384,128]{2,1,0:T(8,128)} %get-tuple-element.20), channel_id=1, source_target_pairs={{0,1},{2,3},{4,5},{6,7},{8,9},{10,11},{12,13},{14,15},{16,17},{18,... | collective-permute-start | bytes 1179656 | tf_op jit(solution)/shard_map/ppermute | solution.py:171
  87.5 11.6 %collective-permute-start.7 = (f32[2,384,128]{2,1,0:T(8,128)}, f32[2,384,128]{2,1,0:T(8,128)}, u32[]{:S(2)}, u32[]{:S(2)}) collective-permute-start(f32[2,384,128]{2,1,0:T(8,128)} %get-tuple-element.21), channel_id=1, source_target_pairs={{1,2},{3,4},{5,6},{7,8},{9,10},{11,12},{13,14},{15,16},{17,18},{19... | collective-permute-start | bytes 1179656 | tf_op jit(solution)/shard_map/ppermute | solution.py:171
  94.1 10.1 %all-to-all-start.2 = ((f32[16,40,128]{2,1,0:T(8,128)}), f32[16,40,128]{2,1,0:T(8,128)S(1)}, u32[]{:S(2)}, u32[]{:S(2)}) async-start(f32[16,40,128]{2,1,0:T(8,128)} %broadcast_in_dim.23), calls=%async_computation.2 | async-start | bytes 655360 | tf_op jit(solution)/shard_map/all_to_all | solution.py:198
  104.2 6.7 %collective-permute-start.9 = (f32[640,128]{1,0:T(8,128)S(1)}, f32[640,128]{1,0:T(8,128)S(1)}, u32[]{:S(2)}, u32[]{:S(2)}) collective-permute-start(f32[640,128]{1,0:T(8,128)S(1)} %bitcast.16), channel_id=1, source_target_pairs={{0,1},{1,0},{2,3},{3,2},{4,5},{5,4},{6,7},{7,6},{8,9},{9,8},{10,11... | collective-permute-start | bytes 983048 | tf_op jit(solution)/shard_map/ppermute | solution.py:207
  109.2 1.7 copy-start.4
  109.2 1.7 copy-start.6
  109.3 1.7 copy-start.8
  121.2 1.7 collective-permute-start.14
  123.6 20.6 %all-to-all-start.3 = ((f32[16,40,128]{2,1,0:T(8,128)}), f32[16,40,128]{2,1,0:T(8,128)S(1)}, u32[]{:S(2)}, u32[]{:S(2)}) async-start(f32[16,40,128]{2,1,0:T(8,128)} %bitcast.7), calls=%async_computation.3 | async-start | bytes 655360 | tf_op jit(solution)/shard_map/all_to_all | solution.py:198
  137.4 12.3 %collective-permute-start.10 = (f32[2,64,384]{2,1,0:T(8,128)S(1)}, f32[2,64,384]{2,1,0:T(8,128)S(1)}, u32[]{:S(2)}, u32[]{:S(2)}) collective-permute-start(f32[2,64,384]{2,1,0:T(8,128)S(1)} %get-tuple-element.16), channel_id=1, source_target_pairs={{0,32},{64,96},{128,160},{192,224},{32,0},{96,64},{160,128},{224,1... | collective-permute-start | bytes 589832 | tf_op jit(solution)/shard_map/ppermute | solution.py:171
  138.8 10.8 %collective-permute-start.11 = (f32[2,64,384]{2,1,0:T(8,128)S(1)}, f32[2,64,384]{2,1,0:T(8,128)S(1)}, u32[]{:S(2)}, u32[]{:S(2)}) collective-permute-start(f32[2,64,384]{2,1,0:T(8,128)S(1)} %get-tuple-element.17), channel_id=1, source_target_pairs={{32,64},{96,128},{160,192},{64,32},{128,96},{192,160},{33,65},{97,... | collective-permute-start | bytes 589832 | tf_op jit(solution)/shard_map/ppermute | solution.py:171
  145.0 14.1 %all-to-all-start.4 = ((f32[8,40,128]{2,1,0:T(8,128)}), f32[8,40,128]{2,1,0:T(8,128)S(1)}, u32[]{:S(2)}, u32[]{:S(2)}) async-start(f32[8,40,128]{2,1,0:T(8,128)} %broadcast_in_dim.40), calls=%async_computation.4 | async-start | bytes 327680 | tf_op jit(solution)/shard_map/all_to_all | solution.py:198
  159.8 10.7 %all-to-all-start.5 = ((f32[16,40,128]{2,1,0:T(8,128)}), f32[16,40,128]{2,1,0:T(8,128)S(1)}, u32[]{:S(2)}, u32[]{:S(2)}) async-start(f32[16,40,128]{2,1,0:T(8,128)} %broadcast_in_dim.41), calls=%async_computation.5 | async-start | bytes 655360 | tf_op jit(solution)/shard_map/all_to_all | solution.py:198
  164.8 9.6 %collective-permute-start.12 = (f32[2,256,64]{2,1,0:T(8,128)S(1)}, f32[2,256,64]{2,1,0:T(8,128)S(1)}, u32[]{:S(2)}, u32[]{:S(2)}) collective-permute-start(f32[2,256,64]{2,1,0:T(8,128)S(1)} %get-tuple-element.22), channel_id=1, source_target_pairs={{0,1},{2,3},{4,5},{6,7},{8,9},{10,11},{12,13},{14,15},{16,17},{18,... | collective-permute-start | bytes 393224 | tf_op jit(solution)/shard_map/ppermute | solution.py:171
  167.9 9.8 %collective-permute-start.13 = (f32[2,256,64]{2,1,0:T(8,128)S(1)}, f32[2,256,64]{2,1,0:T(8,128)S(1)}, u32[]{:S(2)}, u32[]{:S(2)}) collective-permute-start(f32[2,256,64]{2,1,0:T(8,128)S(1)} %get-tuple-element.23), channel_id=1, source_target_pairs={{1,2},{3,4},{5,6},{7,8},{9,10},{11,12},{13,14},{15,16},{17,18},{19... | collective-permute-start | bytes 393224 | tf_op jit(solution)/shard_map/ppermute | solution.py:171
  170.5 9.4 %collective-permute-start.15 = (f32[640,128]{1,0:T(8,128)S(1)}, f32[640,128]{1,0:T(8,128)S(1)}, u32[]{:S(2)}, u32[]{:S(2)}) collective-permute-start(f32[640,128]{1,0:T(8,128)S(1)} %bitcast.19), channel_id=1, source_target_pairs={{0,1},{1,0},{2,3},{3,2},{4,5},{5,4},{6,7},{7,6},{8,9},{9,8},{10,11... | collective-permute-start | bytes 983048 | tf_op jit(solution)/shard_map/ppermute | solution.py:207
  (14 other events, 19.1 us)
